TPU v7x, 256 devices: a whole 4x4x8 slice. The times are simulated.
256 devices in a mesh: ctx: 32 (over y, x, core), seq: 8 (over z).
Axes of the slice: x: 4, y: 4, z: 8, core: 2. Of those that a mesh axis runs over, the one named last changes fastest.
Arguments:
- queries: bfloat16 [32768, 4096], P(('seq', 'ctx')), may hold values from -6 to 6
- key_proj: bfloat16 [32768, 4096], P(('seq', 'ctx')), may hold values from -6 to 6
- value_proj: bfloat16 [32768, 4096], P(('seq', 'ctx')), may hold values from -6 to 6
- decay_rate: float32 [16, 4096], P(None, 'ctx'), may hold values from 3.0517578e-06 to 0.06
- residue: float32 [16, 4096], P(None, 'ctx'), may hold values from -1 to 1
- skip_gain: float32 [4096], P('ctx'), may hold values from -1 to 1
Outputs:
- operator_out: bfloat16 [32768, 4096], P(('seq', 'ctx'))
All inputs are finite; a program needn't handle non-finite values.
Results may differ from a plain program's by a relative error of at most 0.011.
Values may be sent and summed in bfloat16 or wider, within the bound.
No kernel may reach another device: no remote copies, remote signals or barrier semaphores. Data moves between devices by JAX's collectives and lax.ppermute only.
A program may use at most 320 MiB of HBM per device.

v0:
```python
import jax
import jax.numpy as jnp
from jax import lax
from jax.experimental import pallas as pl
from jax.experimental.pallas import tpu as pltpu
from jax.sharding import PartitionSpec as P

F32, BF16 = jnp.float32, jnp.bfloat16
LANES = 128
SUB = 8
WIDE = SUB * LANES
CHUNK = 128
MODES = 16
ROWS = 2 * MODES + SUB
TABLE = 2 * MODES + 1


def one_minus_exp(x):
    series = jnp.ones_like(x)
    for order in range(9, 1, -1):
        series = 1.0 - x * (1.0 / order) * series
    return jnp.where(x < 0.5, x * series, 1.0 - jnp.exp(-x))


def table_kernel(rate_ref, resid_ref, gain_ref, out_ref):
    rate = rate_ref[...]
    weight = resid_ref[...] * jnp.sqrt(one_minus_exp(2.0 * rate))
    gain = jnp.broadcast_to(gain_ref[...], (SUB, LANES))
    rows = jnp.concatenate([rate, weight, gain], axis=0).astype(BF16)
    for d in range(out_ref.shape[0]):
        out_ref[d] = rows


def mix_kernel(k_ref, v_ref, out_ref):
    for g in range(SUB):
        cols = slice(g * LANES, (g + 1) * LANES)
        mixed = k_ref[:, cols].astype(F32) * v_ref[:, cols].astype(F32)
        out_ref[pl.ds(g, CHUNK, stride=SUB), :] = mixed.astype(BF16).astype(F32)


def chunk_kernel(x_ref, par_ref, end_ref, table_ref, rows, ends):
    for g in range(SUB):
        rows[g * ROWS : g * ROWS + ROWS, :] = par_ref[g].astype(F32)
    powers = []
    for m in range(MODES):
        power = jnp.exp(-rows[pl.ds(m, SUB, stride=ROWS), :])
        powers.append(power)
        table_ref[m * SUB : (m + 1) * SUB, :] = power
        table_ref[(MODES + m) * SUB : (MODES + m + 1) * SUB, :] = rows[
            pl.ds(MODES + m, SUB, stride=ROWS), :
        ]
    table_ref[2 * MODES * SUB :, :] = rows[pl.ds(2 * MODES, SUB, stride=ROWS), :]

    def token(t, states):
        x = x_ref[pl.ds(pl.multiple_of(t * SUB, SUB), SUB), :]
        return tuple(powers[m] * states[m] + x for m in range(MODES))

    zero = jnp.zeros((SUB, LANES), F32)
    states = lax.fori_loop(0, CHUNK, token, (zero,) * MODES, unroll=8)
    for m in range(MODES):
        ends[pl.ds(m, SUB, stride=MODES), :] = states[m]
    for g in range(SUB):
        end_ref[g] = ends[g * MODES : (g + 1) * MODES, :].astype(BF16)


def tree_sum(terms):
    while len(terms) > 1:
        terms = [terms[i] + terms[i + 1] for i in range(0, len(terms), 2)]
    return terms[0]


def inner_kernel(x_ref, table_ref, y_ref):
    powers = [table_ref[m * SUB : (m + 1) * SUB, :] for m in range(MODES)]
    weights = [table_ref[(MODES + m) * SUB : (MODES + m + 1) * SUB, :] for m in range(MODES)]
    gain = table_ref[2 * MODES * SUB :, :]

    def token(t, states):
        at = pl.ds(pl.multiple_of(t * SUB, SUB), SUB)
        x = x_ref[at, :]
        states = tuple(powers[m] * states[m] + x for m in range(MODES))
        y_ref[at, :] = gain * x + tree_sum([weights[m] * states[m] for m in range(MODES)])
        return states

    zero = jnp.zeros((SUB, LANES), F32)
    lax.fori_loop(0, CHUNK, token, (zero,) * MODES, unroll=4)


def block_kernel(ends_ref, rate_ref, before_ref, end_ref):
    decay = jnp.exp(-float(CHUNK) * rate_ref[...])
    state = jnp.zeros((MODES, LANES), F32)
    for d in range(before_ref.shape[0]):
        before_ref[d] = state
        state = decay * state + ends_ref[d].astype(F32)
    for z in range(end_ref.shape[0]):
        end_ref[z] = state


def link_kernel(place_ref, before_ref, blocks_ref, rate_ref, out_ref):
    nchunks = before_ref.shape[0]
    place = place_ref[0]
    span = jnp.exp(-float(CHUNK * nchunks) * rate_ref[...])
    start = jnp.zeros((MODES, LANES), F32)
    for z in range(blocks_ref.shape[0]):
        start = jnp.where(z < place, span * start + blocks_ref[z], start)
    decay = jnp.exp(-float(CHUNK) * rate_ref[...])
    for d in range(nchunks):
        out_ref[d] = (before_ref[d] + start).astype(BF16)
        start = decay * start


def final_kernel(start_ref, table_ref, y_ref, q_ref, out_ref, rows, pre):
    for g in range(SUB):
        rows[g * MODES : (g + 1) * MODES, :] = start_ref[g].astype(F32)
    powers = [table_ref[m * SUB : (m + 1) * SUB, :] for m in range(MODES)]
    terms = tuple(
        table_ref[(MODES + m) * SUB : (MODES + m + 1) * SUB, :]
        * powers[m]
        * rows[pl.ds(m, SUB, stride=MODES), :]
        for m in range(MODES)
    )

    def token(t, terms):
        at = pl.ds(pl.multiple_of(t * SUB, SUB), SUB)
        pre[at, :] = y_ref[at, :] + tree_sum(list(terms))
        return tuple(terms[m] * powers[m] for m in range(MODES))

    lax.fori_loop(0, CHUNK, token, terms, unroll=8)
    for g in range(SUB):
        cols = slice(g * LANES, (g + 1) * LANES)
        gate = pre[pl.ds(g, CHUNK, stride=SUB), :].astype(BF16).astype(F32)
        out_ref[:, cols] = (q_ref[:, cols].astype(F32) * gate).astype(BF16)


def local(queries, key_proj, value_proj, decay_rate, residue, skip_gain, *, interpret=False):
    tokens, channels = queries.shape
    groups = channels // LANES
    grid = channels // WIDE
    nseq = lax.axis_size("seq")

    def call(kernel, name, flops, nbytes, **kw):
        return pl.pallas_call(
            kernel,
            name=name,
            cost_estimate=pl.CostEstimate(flops=flops, bytes_accessed=nbytes, transcendentals=0),
            interpret=interpret,
            **kw,
        )

    def exchange(array, axis):
        return lax.all_to_all(array, axis, split_axis=0, concat_axis=0, tiled=True)

    struct = jax.ShapeDtypeStruct
    tight = pltpu.CompilerParams(vmem_limit_bytes=16 * 1024 * 1024)
    cols = pl.BlockSpec((CHUNK, WIDE), lambda i: (0, i))
    rows = pl.BlockSpec((CHUNK * SUB, LANES), lambda i: (i, 0))
    modes = pl.BlockSpec((SUB, MODES, LANES), lambda i: (i, 0, 0))
    tables = pl.BlockSpec((TABLE * SUB, LANES), lambda i: (i, 0))
    signal = struct((grid * CHUNK * SUB, LANES), F32)

    params = call(
        table_kernel, "table", 1_000_000, 400_000,
        out_shape=struct((groups, ROWS, LANES), BF16),
    )(decay_rate, residue, skip_gain[None, :])
    params = exchange(params, "ctx")

    mixed = call(
        mix_kernel, "mix", 2_000_000_000, 4_000_000,
        grid=(grid,), in_specs=[cols, cols], out_specs=rows, out_shape=signal,
    )(key_proj, value_proj)

    ends, table = call(
        chunk_kernel, "chunk", 20_000_000, 3_000_000,
        grid=(grid,),
        in_specs=[rows, pl.BlockSpec((SUB, ROWS, LANES), lambda i: (i, 0, 0))],
        out_specs=[modes, tables],
        out_shape=[struct((groups, MODES, LANES), BF16), struct((grid * TABLE * SUB, LANES), F32)],
        scratch_shapes=[
            pltpu.VMEM((SUB * ROWS, LANES), F32),
            pltpu.VMEM((SUB * MODES, LANES), F32),
        ],
    )(mixed, params)
    ends = exchange(ends, "ctx")

    before, end_state = call(
        block_kernel, "block", 300_000, 500_000,
        out_shape=[struct((groups, MODES, LANES), F32), struct((nseq, MODES, LANES), F32)],
        compiler_params=tight,
    )(ends, decay_rate)
    blocks = exchange(end_state, "seq")

    inner = call(
        inner_kernel, "inner", 2_000_000_000, 5_000_000,
        grid=(grid,), in_specs=[rows, tables], out_specs=rows, out_shape=signal,
    )(mixed, table)

    starts = call(
        link_kernel, "link", 300_000, 500_000,
        in_specs=[pl.BlockSpec(memory_space=pltpu.SMEM)] + [pl.BlockSpec(memory_space=pltpu.VMEM)] * 3,
        out_shape=struct((groups, MODES, LANES), BF16),
        compiler_params=tight,
    )(lax.axis_index("seq").astype(jnp.int32)[None], before, blocks, decay_rate)
    starts = exchange(starts, "ctx")

    return call(
        final_kernel, "final", 20_000_000, 5_000_000,
        grid=(grid,),
        in_specs=[modes, tables, rows, cols],
        out_specs=cols,
        out_shape=struct((tokens, channels), BF16),
        scratch_shapes=[
            pltpu.VMEM((SUB * MODES, LANES), F32),
            pltpu.VMEM((CHUNK * SUB, LANES), F32),
        ],
    )(starts, table, inner, queries)


def solution(mesh):
    rows = P(("seq", "ctx"), None)
    return jax.shard_map(
        local,
        mesh=mesh,
        in_specs=(rows, rows, rows, P(None, "ctx"), P(None, "ctx"), P("ctx")),
        out_specs=rows,
        check_vma=False,
    )
```

profile of v0, /device:TPU:1, one launch (start us, length us, event | category | flops | bytes accessed | tf_op | source)
XLA Modules:
  0.0 72.9 jit_solution(9020063916932027716)
XLA Ops:
  0.0 1.5 %table.1 = bf16[32,40,128]{2,1,0:T(8,128)(2,1)} custom-call(f32[16,128]{1,0:T(8,128)} %rate_ref.5, f32[16,128]{1,0:T(8,128)} %resid_ref.1, f32[1,128]{1,0:T(1,128)} %bitcast.2), custom_call_target="tpu_custom_call" | custom-call | flops 1000000 | bytes 400000 | tf_op jit(solution)/shard_map/table/pallas_call | solution.py:160
  1.5 8.6 %all-to-all-start = ((bf16[32,40,128]{2,1,0:T(8,128)(2,1)}), bf16[32,40,128]{2,1,0:T(8,128)(2,1)S(1)}, u32[]{:S(2)}, u32[]{:S(2)}) async-start(bf16[32,40,128]{2,1,0:T(8,128)(2,1)} %table.1), calls=%async_computation | async-start | bytes 655360 | tf_op jit(solution)/shard_map/all_to_all | solution.py:150
  10.1 4.0 %mix.1.x_ref = f32[4096,128]{1,0:T(8,128)} custom-call(bf16[128,4096]{1,0:T(8,128)(2,1)} %k_ref.1, bf16[128,4096]{1,0:T(8,128)(2,1)} %v_ref.1), custom_call_target="tpu_custom_call" | custom-call | flops 2000000000 | bytes 4000000 | tf_op jit(solution)/shard_map/mix/pallas_call | solution.py:166
  14.0 0.0 copy-start
  14.0 5.6 %all-to-all-done.par_ref = bf16[32,40,128]{2,1,0:T(8,128)(2,1)S(1)} async-done(((bf16[32,40,128]{2,1,0:T(8,128)(2,1)}), bf16[32,40,128]{2,1,0:T(8,128)(2,1)S(1)}, u32[]{:S(2)}, u32[]{:S(2)}) %all-to-all-start) | async-done | bytes 327712 | tf_op jit(solution)/shard_map/all_to_all | solution.py:150
  19.6 0.0 copy-start.1
  19.6 0.7 copy-done.1
  20.3 4.9 %chunk.1 = (bf16[32,16,128]{2,1,0:T(8,128)(2,1)}, f32[1056,128]{1,0:T(8,128)}) custom-call(f32[4096,128]{1,0:T(8,128)} %mix.1.x_ref, bf16[32,40,128]{2,1,0:T(8,128)(2,1)} %copy-done.1), custom_call_target="tpu_custom_call" | custom-call | flops 20000000 | bytes 3000000 | tf_op jit(solution)/shard_map/chunk/pallas_call | solution.py:171
  25.2 11.5 %all_to_all.20.ends_ref = bf16[32,16,128]{2,1,0:T(8,128)(2,1)S(1)} all-to-all(bf16[32,16,128]{2,1,0:T(8,128)(2,1)} %get-tuple-element.9), channel_id=1, replica_groups=mesh['ctx'=32,'seq'=8] {'ctx'}, dimensions={0} | all-to-all | bytes 262144 | tf_op jit(solution)/shard_map/all_to_all | solution.py:150
  36.8 0.0 copy-done
  36.8 0.7 block.1
  37.5 8.2 %all-to-all-start.2 = ((f32[8,16,128]{2,1,0:T(8,128)}), f32[8,16,128]{2,1,0:T(8,128)S(1)}, u32[]{:S(2)}, u32[]{:S(2)}) async-start(f32[8,16,128]{2,1,0:T(8,128)} %get-tuple-element.11), calls=%async_computation.2 | async-start | bytes 131072 | tf_op jit(solution)/shard_map/all_to_all | solution.py:150
  45.7 7.2 %all-to-all-done.2.blocks_ref = f32[8,16,128]{2,1,0:T(8,128)S(1)} async-done(((f32[8,16,128]{2,1,0:T(8,128)}), f32[8,16,128]{2,1,0:T(8,128)S(1)}, u32[]{:S(2)}, u32[]{:S(2)}) %all-to-all-start.2) | async-done | bytes 65568 | tf_op jit(solution)/shard_map/all_to_all | solution.py:150
  52.9 0.7 link.1
  53.6 5.3 %all-to-all-start.3 = ((bf16[32,16,128]{2,1,0:T(8,128)(2,1)}), bf16[32,16,128]{2,1,0:T(8,128)(2,1)S(1)}, u32[]{:S(2)}, u32[]{:S(2)}) async-start(bf16[32,16,128]{2,1,0:T(8,128)(2,1)} %link.1), calls=%async_computation.3 | async-start | bytes 262144 | tf_op jit(solution)/shard_map/all_to_all | solution.py:150
  59.0 6.9 %inner.1.y_ref = f32[4096,128]{1,0:T(8,128)} custom-call(f32[4096,128]{1,0:T(8,128)} %mix.1.x_ref, f32[1056,128]{1,0:T(8,128)} %get-tuple-element.12.table_ref), custom_call_target="tpu_custom_call" | custom-call | flops 2000000000 | bytes 5000000 | tf_op jit(solution)/shard_map/inner/pallas_call | solution.py:191
  65.9 0.8 %all-to-all-done.3.start_ref = bf16[32,16,128]{2,1,0:T(8,128)(2,1)S(1)} async-done(((bf16[32,16,128]{2,1,0:T(8,128)(2,1)}), bf16[32,16,128]{2,1,0:T(8,128)(2,1)S(1)}, u32[]{:S(2)}, u32[]{:S(2)}) %all-to-all-start.3) | async-done | bytes 131104 | tf_op jit(solution)/shard_map/all_to_all | solution.py:150
  66.7 0.0 copy-start.2
  66.7 0.6 copy-done.2
  67.4 5.5 %final.1 = bf16[128,4096]{1,0:T(8,128)(2,1)} custom-call(bf16[32,16,128]{2,1,0:T(8,128)(2,1)} %copy-done.2, f32[1056,128]{1,0:T(8,128)} %get-tuple-element.12.table_ref, f32[4096,128]{1,0:T(8,128)} %inner.1.y_ref, bf16[128,4096]{1,0:T(8,128)(2,1)} %q_ref.1), custom_call_target="tpu_custom_call" | custom-call | flops 20000000 | bytes 5000000 | tf_op jit(solution)/shard_map/final/pallas_call | solution.py:204
Async XLA Ops:
  1.5 18.1 %all-to-all-start = ((bf16[32,40,128]{2,1,0:T(8,128)(2,1)}), bf16[32,40,128]{2,1,0:T(8,128)(2,1)S(1)}, u32[]{:S(2)}, u32[]{:S(2)}) async-start(bf16[32,40,128]{2,1,0:T(8,128)(2,1)} %table.1), calls=%async_computation | async-start | bytes 655360 | tf_op jit(solution)/shard_map/all_to_all | solution.py:150
  14.0 22.7 %copy-start = (f32[16,128]{1,0:T(8,128)S(1)}, f32[16,128]{1,0:T(8,128)}, u32[]{:S(2)}) copy-start(f32[16,128]{1,0:T(8,128)} %rate_ref.5) | copy-start | bytes 24580
  19.6 0.7 copy-start.1
  37.5 15.4 %all-to-all-start.2 = ((f32[8,16,128]{2,1,0:T(8,128)}), f32[8,16,128]{2,1,0:T(8,128)S(1)}, u32[]{:S(2)}, u32[]{:S(2)}) async-start(f32[8,16,128]{2,1,0:T(8,128)} %get-tuple-element.11), calls=%async_computation.2 | async-start | bytes 131072 | tf_op jit(solution)/shard_map/all_to_all | solution.py:150
  53.6 13.1 %all-to-all-start.3 = ((bf16[32,16,128]{2,1,0:T(8,128)(2,1)}), bf16[32,16,128]{2,1,0:T(8,128)(2,1)S(1)}, u32[]{:S(2)}, u32[]{:S(2)}) async-start(bf16[32,16,128]{2,1,0:T(8,128)(2,1)} %link.1), calls=%async_computation.3 | async-start | bytes 262144 | tf_op jit(solution)/shard_map/all_to_all | solution.py:150
  66.7 0.6 copy-start.2
where the time goes:
time: 73.6 us; the launch traced here: 72.9 us
  Pallas kernels  24.2 us (33%)
  starting transfers between devices  22.1 us (30%)
  waiting for transfers between devices  13.6 us (18%)
  blocking collectives  11.5 us (16%)
  local copies, waits for them, and re-layouts  1.37 us (2%)
    all_to_all x3, starting transfers between devices, exchange(): return lax.all_to_all(array, axis, split_axis=0, concat_axis=0, tiled=True)  22.1 us
    all_to_all x3, waiting for transfers between devices, exchange(): return lax.all_to_all(array, axis, split_axis=0, concat_axis=0, tiled=True)  13.6 us
    all_to_all x1, blocking collectives, exchange(): return lax.all_to_all(array, axis, split_axis=0, concat_axis=0, tiled=True)  11.5 us
    pallas_call x1, Pallas kernels, local(): call(inner_kernel, 'inner', 2000000000, 5000000, grid=(grid,), in_specs=[...  6.95 us
    pallas_call x1, Pallas kernels, local(): call(final_kernel, 'final', 20000000, 5000000, grid=(grid,), in_specs=[mo...  5.52 us
    pallas_call x1, Pallas kernels, local(): call(chunk_kernel, 'chunk', 20000000, 3000000, grid=(grid,), in_specs=[ro...  4.9 us
    pallas_call x1, Pallas kernels, local(): call(mix_kernel, 'mix', 2000000000, 4000000, grid=(grid,), in_specs=[cols...  3.96 us
    pallas_call x1, Pallas kernels, local(): call(table_kernel, 'table', 1000000, 400000, out_shape=struct((groups, RO...  1.48 us
  transfers between devices with their start and end apart: 3, of which 3 were waited for; matrix products, arithmetic and copies ran while one was open for 0% of the time, Pallas kernels for 15%

commit v1 on v0

--- a/solution.py
+++ b/solution.py
@@ -12,7 +12,6 @@
 CHUNK = 128
 MODES = 16
 ROWS = 2 * MODES + SUB
-TABLE = 2 * MODES + 1
 
 
 def one_minus_exp(x):
@@ -38,29 +37,27 @@
         out_ref[pl.ds(g, CHUNK, stride=SUB), :] = mixed.astype(BF16).astype(F32)
 
 
-def chunk_kernel(x_ref, par_ref, end_ref, table_ref, rows, ends):
-    for g in range(SUB):
-        rows[g * ROWS : g * ROWS + ROWS, :] = par_ref[g].astype(F32)
-    powers = []
-    for m in range(MODES):
-        power = jnp.exp(-rows[pl.ds(m, SUB, stride=ROWS), :])
-        powers.append(power)
-        table_ref[m * SUB : (m + 1) * SUB, :] = power
-        table_ref[(MODES + m) * SUB : (MODES + m + 1) * SUB, :] = rows[
-            pl.ds(MODES + m, SUB, stride=ROWS), :
-        ]
-    table_ref[2 * MODES * SUB :, :] = rows[pl.ds(2 * MODES, SUB, stride=ROWS), :]
-
-    def token(t, states):
-        x = x_ref[pl.ds(pl.multiple_of(t * SUB, SUB), SUB), :]
-        return tuple(powers[m] * states[m] + x for m in range(MODES))
-
-    zero = jnp.zeros((SUB, LANES), F32)
-    states = lax.fori_loop(0, CHUNK, token, (zero,) * MODES, unroll=8)
-    for m in range(MODES):
-        ends[pl.ds(m, SUB, stride=MODES), :] = states[m]
-    for g in range(SUB):
-        end_ref[g] = ends[g * MODES : (g + 1) * MODES, :].astype(BF16)
+def spread(par_ref, first, rows):
+    for g in range(SUB):
+        rows[g * ROWS : g * ROWS + ROWS, :] = par_ref[first + g].astype(F32)
+
+
+def chunk_kernel(x_ref, par_ref, end_ref, rows, ends):
+    for wide in range(x_ref.shape[0] // (CHUNK * SUB)):
+        place = wide * CHUNK * SUB
+        spread(par_ref, wide * SUB, rows)
+        powers = [jnp.exp(-rows[pl.ds(m, SUB, stride=ROWS), :]) for m in range(MODES)]
+
+        def token(t, states):
+            x = x_ref[pl.ds(pl.multiple_of(place + t * SUB, SUB), SUB), :]
+            return tuple(powers[m] * states[m] + x for m in range(MODES))
+
+        zero = jnp.zeros((SUB, LANES), F32)
+        states = lax.fori_loop(0, CHUNK, token, (zero,) * MODES, unroll=8)
+        for m in range(MODES):
+            ends[pl.ds(m, SUB, stride=MODES), :] = states[m]
+        for g in range(SUB):
+            end_ref[wide * SUB + g] = ends[g * MODES : (g + 1) * MODES, :].astype(BF16)
 
 
 def tree_sum(terms):
@@ -69,10 +66,11 @@
     return terms[0]
 
 
-def inner_kernel(x_ref, table_ref, y_ref):
-    powers = [table_ref[m * SUB : (m + 1) * SUB, :] for m in range(MODES)]
-    weights = [table_ref[(MODES + m) * SUB : (MODES + m + 1) * SUB, :] for m in range(MODES)]
-    gain = table_ref[2 * MODES * SUB :, :]
+def inner_kernel(x_ref, par_ref, y_ref, rows):
+    spread(par_ref, 0, rows)
+    powers = [jnp.exp(-rows[pl.ds(m, SUB, stride=ROWS), :]) for m in range(MODES)]
+    weights = [rows[pl.ds(MODES + m, SUB, stride=ROWS), :] for m in range(MODES)]
+    gain = rows[pl.ds(2 * MODES, SUB, stride=ROWS), :]
 
     def token(t, states):
         at = pl.ds(pl.multiple_of(t * SUB, SUB), SUB)
@@ -108,14 +106,15 @@
         start = decay * start
 
 
-def final_kernel(start_ref, table_ref, y_ref, q_ref, out_ref, rows, pre):
-    for g in range(SUB):
-        rows[g * MODES : (g + 1) * MODES, :] = start_ref[g].astype(F32)
-    powers = [table_ref[m * SUB : (m + 1) * SUB, :] for m in range(MODES)]
+def final_kernel(start_ref, par_ref, y_ref, q_ref, out_ref, rows, starts, pre):
+    spread(par_ref, 0, rows)
+    for g in range(SUB):
+        starts[g * MODES : (g + 1) * MODES, :] = start_ref[g].astype(F32)
+    powers = [jnp.exp(-rows[pl.ds(m, SUB, stride=ROWS), :]) for m in range(MODES)]
     terms = tuple(
-        table_ref[(MODES + m) * SUB : (MODES + m + 1) * SUB, :]
+        rows[pl.ds(MODES + m, SUB, stride=ROWS), :]
         * powers[m]
-        * rows[pl.ds(m, SUB, stride=MODES), :]
+        * starts[pl.ds(m, SUB, stride=MODES), :]
         for m in range(MODES)
     )
 
@@ -154,7 +153,7 @@
     cols = pl.BlockSpec((CHUNK, WIDE), lambda i: (0, i))
     rows = pl.BlockSpec((CHUNK * SUB, LANES), lambda i: (i, 0))
     modes = pl.BlockSpec((SUB, MODES, LANES), lambda i: (i, 0, 0))
-    tables = pl.BlockSpec((TABLE * SUB, LANES), lambda i: (i, 0))
+    tables = pl.BlockSpec((SUB, ROWS, LANES), lambda i: (i, 0, 0))
     signal = struct((grid * CHUNK * SUB, LANES), F32)
 
     params = call(
@@ -165,19 +164,19 @@
 
     mixed = call(
         mix_kernel, "mix", 2_000_000_000, 4_000_000,
-        grid=(grid,), in_specs=[cols, cols], out_specs=rows, out_shape=signal,
+        grid=(grid,), in_specs=[cols, cols], out_specs=rows, out_shape=signal, compiler_params=tight,
     )(key_proj, value_proj)
 
-    ends, table = call(
+    ends = call(
         chunk_kernel, "chunk", 20_000_000, 3_000_000,
-        grid=(grid,),
-        in_specs=[rows, pl.BlockSpec((SUB, ROWS, LANES), lambda i: (i, 0, 0))],
-        out_specs=[modes, tables],
-        out_shape=[struct((groups, MODES, LANES), BF16), struct((grid * TABLE * SUB, LANES), F32)],
+        in_specs=[pl.BlockSpec(memory_space=pltpu.VMEM)] * 2,
+        out_specs=pl.BlockSpec(memory_space=pltpu.VMEM),
+        out_shape=struct((groups, MODES, LANES), BF16),
         scratch_shapes=[
             pltpu.VMEM((SUB * ROWS, LANES), F32),
             pltpu.VMEM((SUB * MODES, LANES), F32),
         ],
+        compiler_params=tight,
     )(mixed, params)
     ends = exchange(ends, "ctx")
 
@@ -190,8 +189,13 @@
 
     inner = call(
         inner_kernel, "inner", 2_000_000_000, 5_000_000,
-        grid=(grid,), in_specs=[rows, tables], out_specs=rows, out_shape=signal,
-    )(mixed, table)
+        grid=(grid,),
+        in_specs=[rows, tables],
+        out_specs=rows,
+        out_shape=pltpu.HBM(signal.shape, F32),
+        scratch_shapes=[pltpu.VMEM((SUB * ROWS, LANES), F32)],
+        compiler_params=tight,
+    )(mixed, params)
 
     starts = call(
         link_kernel, "link", 300_000, 500_000,
@@ -208,10 +212,12 @@
         out_specs=cols,
         out_shape=struct((tokens, channels), BF16),
         scratch_shapes=[
+            pltpu.VMEM((SUB * ROWS, LANES), F32),
             pltpu.VMEM((SUB * MODES, LANES), F32),
             pltpu.VMEM((CHUNK * SUB, LANES), F32),
         ],
-    )(starts, table, inner, queries)
+        compiler_params=tight,
+    )(starts, params, pltpu.with_memory_space_constraint(inner, pltpu.HBM), queries)
 
 
 def solution(mesh):

time: 73.6 us -> 69.9 us (0.950)
  Pallas kernels: 24.2 us -> 17.6 us
  waiting for transfers between devices: 13.6 us -> 15.3 us
  local copies, waits for them, and re-layouts: 1.37 us -> 2.46 us
    pallas_call x1, Pallas kernels: 3.96 us -> 0.71 us  [local(): call(mix_kernel, 'mix', 2000000000, 4000000, grid=(grid,), in_specs=[cols...]
    pallas_call x1, Pallas kernels: 4.9 us -> 2.58 us  [local(): call(chunk_kernel, 'chunk', 20000000, 3000000, in_specs=[pl.BlockSpec(mem...]
    all_to_all x3, waiting for transfers between devices: 13.6 us -> 15.3 us  [exchange(): return lax.all_to_all(array, axis, split_axis=0, concat_axis=0, tiled=True)]
    unnamed x6 -> x8, local copies, waits for them, and re-layouts: 1.37 us -> 2.46 us
    pallas_call x1, Pallas kernels: 6.95 us -> 6.02 us  [local(): call(inner_kernel, 'inner', 2000000000, 5000000, grid=(grid,), in_specs=[...]
  transfers between devices with their start and end apart: 3 -> 3, of which waited for: 3 -> 3; matrix products, arithmetic and copies ran while one was open for 0% -> 0% of each run, Pallas kernels for 15% -> 10%
where the time goes in v1:
time: 69.9 us; the launch traced here: 69.4 us
  starting transfers between devices  22.8 us (33%)
  Pallas kernels  17.6 us (25%)
  waiting for transfers between devices  15.3 us (22%)
  blocking collectives  11.2 us (16%)
  local copies, waits for them, and re-layouts  2.46 us (4%)
    all_to_all x3, starting transfers between devices, exchange(): return lax.all_to_all(array, axis, split_axis=0, concat_axis=0, tiled=True)  22.8 us
    all_to_all x3, waiting for transfers between devices, exchange(): return lax.all_to_all(array, axis, split_axis=0, concat_axis=0, tiled=True)  15.3 us
    all_to_all x1, blocking collectives, exchange(): return lax.all_to_all(array, axis, split_axis=0, concat_axis=0, tiled=True)  11.2 us
    pallas_call x1, Pallas kernels, local(): call(inner_kernel, 'inner', 2000000000, 5000000, grid=(grid,), in_specs=[...  6.02 us
    pallas_call x1, Pallas kernels, local(): call(final_kernel, 'final', 20000000, 5000000, grid=(grid,), in_specs=[mo...  5.33 us
    pallas_call x1, Pallas kernels, local(): call(chunk_kernel, 'chunk', 20000000, 3000000, in_specs=[pl.BlockSpec(mem...  2.58 us
    unnamed x8, local copies, waits for them, and re-layouts  2.46 us
    pallas_call x1, Pallas kernels, local(): call(table_kernel, 'table', 1000000, 400000, out_shape=struct((groups, RO...  1.48 us
  transfers between devices with their start and end apart: 3, of which 3 were waited for; matrix products, arithmetic and copies ran while one was open for 0% of the time, Pallas kernels for 10%

profile of v1, /device:TPU:1, one launch (start us, length us, event | category | flops | bytes accessed | tf_op | source)
XLA Modules:
  0.0 69.4 jit_solution(2673790024274742848)
XLA Ops:
  0.0 1.5 %table.1 = bf16[32,40,128]{2,1,0:T(8,128)(2,1)} custom-call(f32[16,128]{1,0:T(8,128)} %rate_ref.5, f32[16,128]{1,0:T(8,128)} %resid_ref.1, f32[1,128]{1,0:T(1,128)} %bitcast.2), custom_call_target="tpu_custom_call" | custom-call | flops 1000000 | bytes 400000 | tf_op jit(solution)/shard_map/table/pallas_call | solution.py:159
  1.5 8.6 %all-to-all-start = ((bf16[32,40,128]{2,1,0:T(8,128)(2,1)}), bf16[32,40,128]{2,1,0:T(8,128)(2,1)S(1)}, u32[]{:S(2)}, u32[]{:S(2)}) async-start(bf16[32,40,128]{2,1,0:T(8,128)(2,1)} %table.1), calls=%async_computation | async-start | bytes 655360 | tf_op jit(solution)/shard_map/all_to_all | solution.py:149
  10.1 0.0 copy-start.2
  10.1 1.2 %copy-done.2 = bf16[128,4096]{1,0:T(8,128)(2,1)S(1)} copy-done((bf16[128,4096]{1,0:T(8,128)(2,1)S(1)}, bf16[128,4096]{1,0:T(8,128)(2,1)}, u32[]{:S(2)}) %copy-start.2) | copy-done | bytes 1048600
  11.3 0.0 copy-start.3
  11.3 1.2 %copy-done.3 = bf16[128,4096]{1,0:T(8,128)(2,1)S(1)} copy-done((bf16[128,4096]{1,0:T(8,128)(2,1)S(1)}, bf16[128,4096]{1,0:T(8,128)(2,1)}, u32[]{:S(2)}) %copy-start.3) | copy-done | bytes 1048600
  12.5 0.7 %mix.1.x_ref = f32[4096,128]{1,0:T(8,128)S(1)} custom-call(bf16[128,4096]{1,0:T(8,128)(2,1)S(1)} %copy-done.2, bf16[128,4096]{1,0:T(8,128)(2,1)S(1)} %copy-done.3), custom_call_target="tpu_custom_call" | custom-call | flops 2000000000 | bytes 4000000 | tf_op jit(solution)/shard_map/mix/pallas_call | solution.py:165
  13.2 0.0 copy-start.1
  13.3 6.4 %all-to-all-done.par_ref = bf16[32,40,128]{2,1,0:T(8,128)(2,1)S(1)} async-done(((bf16[32,40,128]{2,1,0:T(8,128)(2,1)}), bf16[32,40,128]{2,1,0:T(8,128)(2,1)S(1)}, u32[]{:S(2)}, u32[]{:S(2)}) %all-to-all-start) | async-done | bytes 327712 | tf_op jit(solution)/shard_map/all_to_all | solution.py:149
  19.6 2.6 %chunk.1 = bf16[32,16,128]{2,1,0:T(8,128)(2,1)S(1)} custom-call(f32[4096,128]{1,0:T(8,128)S(1)} %mix.1.x_ref, bf16[32,40,128]{2,1,0:T(8,128)(2,1)S(1)} %all-to-all-done.par_ref), custom_call_target="tpu_custom_call" | custom-call | flops 20000000 | bytes 3000000 | tf_op jit(solution)/shard_map/chunk/pallas_call | solution.py:170
  22.2 11.2 %all_to_all.20.ends_ref = bf16[32,16,128]{2,1,0:T(8,128)(2,1)S(1)} all-to-all(bf16[32,16,128]{2,1,0:T(8,128)(2,1)S(1)} %chunk.1), channel_id=1, replica_groups=mesh['ctx'=32,'seq'=8] {'ctx'}, dimensions={0} | all-to-all | bytes 262144 | tf_op jit(solution)/shard_map/all_to_all | solution.py:149
  33.4 0.0 copy-done.1
  33.4 0.7 %block.1 = (f32[32,16,128]{2,1,0:T(8,128)S(1)}, f32[8,16,128]{2,1,0:T(8,128)}) custom-call(bf16[32,16,128]{2,1,0:T(8,128)(2,1)S(1)} %all_to_all.20.ends_ref, f32[16,128]{1,0:T(8,128)S(1)} %copy-done.1), custom_call_target="tpu_custom_call" | custom-call | flops 300000 | bytes 500000 | tf_op jit(solution)/shard_map/block/pallas_call | solution.py:183
  34.1 8.2 %all-to-all-start.2 = ((f32[8,16,128]{2,1,0:T(8,128)}), f32[8,16,128]{2,1,0:T(8,128)S(1)}, u32[]{:S(2)}, u32[]{:S(2)}) async-start(f32[8,16,128]{2,1,0:T(8,128)} %get-tuple-element.8), calls=%async_computation.2 | async-start | bytes 131072 | tf_op jit(solution)/shard_map/all_to_all | solution.py:149
  42.3 7.2 %all-to-all-done.2.blocks_ref = f32[8,16,128]{2,1,0:T(8,128)S(1)} async-done(((f32[8,16,128]{2,1,0:T(8,128)}), f32[8,16,128]{2,1,0:T(8,128)S(1)}, u32[]{:S(2)}, u32[]{:S(2)}) %all-to-all-start.2) | async-done | bytes 65568 | tf_op jit(solution)/shard_map/all_to_all | solution.py:149
  49.5 0.7 %link.1 = bf16[32,16,128]{2,1,0:T(8,128)(2,1)} custom-call(s32[1]{0:T(128)} %bitcast.place_ref, f32[32,16,128]{2,1,0:T(8,128)S(1)} %get-tuple-element.7.before_ref, f32[8,16,128]{2,1,0:T(8,128)S(1)} %all-to-all-done.2.blocks_ref, f32[16,128]{1,0:T(8,128)S(1)} %copy-done.1), custom_call_target="tpu_custom_call" | custom-call | flops 300000 | bytes 500000 | tf_op jit(solution)/shard_map/link/pallas_call | solution.py:200
  50.2 6.0 %all-to-all-start.3 = ((bf16[32,16,128]{2,1,0:T(8,128)(2,1)}), bf16[32,16,128]{2,1,0:T(8,128)(2,1)}, u32[]{:S(2)}, u32[]{:S(2)}) async-start(bf16[32,16,128]{2,1,0:T(8,128)(2,1)} %link.1), calls=%async_computation.3 | async-start | bytes 262144 | tf_op jit(solution)/shard_map/all_to_all | solution.py:149
  56.2 0.0 copy-start
  56.2 6.0 %inner.1.y_ref = f32[4096,128]{1,0:T(8,128)} custom-call(f32[4096,128]{1,0:T(8,128)S(1)} %mix.1.x_ref, bf16[32,40,128]{2,1,0:T(8,128)(2,1)S(1)} %all-to-all-done.par_ref), custom_call_target="tpu_custom_call" | custom-call | flops 2000000000 | bytes 5000000 | tf_op jit(solution)/shard_map/inner/pallas_call | solution.py:190
  62.3 1.8 %all-to-all-done.3.start_ref = bf16[32,16,128]{2,1,0:T(8,128)(2,1)} async-done(((bf16[32,16,128]{2,1,0:T(8,128)(2,1)}), bf16[32,16,128]{2,1,0:T(8,128)(2,1)}, u32[]{:S(2)}, u32[]{:S(2)}) %all-to-all-start.3) | async-done | bytes 131104 | tf_op jit(solution)/shard_map/all_to_all | solution.py:149
  64.0 0.0 copy-done
  64.0 5.3 %final.1 = bf16[128,4096]{1,0:T(8,128)(2,1)} custom-call(bf16[32,16,128]{2,1,0:T(8,128)(2,1)} %all-to-all-done.3.start_ref, bf16[32,40,128]{2,1,0:T(8,128)(2,1)S(1)} %all-to-all-done.par_ref, f32[4096,128]{1,0:T(8,128)} %inner.1.y_ref, bf16[128,4096]{1,0:T(8,128)(2,1)S(1)} %copy-done), custom_call_target="tpu_custom_call" | custom-call | flops 20000000 | bytes 5000000 | tf_op jit(solution)/shard_map/final/pallas_call | solution.py:208
Async XLA Ops:
  1.5 18.1 %all-to-all-start = ((bf16[32,40,128]{2,1,0:T(8,128)(2,1)}), bf16[32,40,128]{2,1,0:T(8,128)(2,1)S(1)}, u32[]{:S(2)}, u32[]{:S(2)}) async-start(bf16[32,40,128]{2,1,0:T(8,128)(2,1)} %table.1), calls=%async_computation | async-start | bytes 655360 | tf_op jit(solution)/shard_map/all_to_all | solution.py:149
  10.1 1.2 %copy-start.2 = (bf16[128,4096]{1,0:T(8,128)(2,1)S(1)}, bf16[128,4096]{1,0:T(8,128)(2,1)}, u32[]{:S(2)}) copy-start(bf16[128,4096]{1,0:T(8,128)(2,1)} %k_ref.1) | copy-start | bytes 3145732
  11.3 1.2 %copy-start.3 = (bf16[128,4096]{1,0:T(8,128)(2,1)S(1)}, bf16[128,4096]{1,0:T(8,128)(2,1)}, u32[]{:S(2)}) copy-start(bf16[128,4096]{1,0:T(8,128)(2,1)} %v_ref.1) | copy-start | bytes 3145732
  13.2 20.1 %copy-start.1 = (f32[16,128]{1,0:T(8,128)S(1)}, f32[16,128]{1,0:T(8,128)}, u32[]{:S(2)}) copy-start(f32[16,128]{1,0:T(8,128)} %rate_ref.5) | copy-start | bytes 24580
  34.1 15.4 %all-to-all-start.2 = ((f32[8,16,128]{2,1,0:T(8,128)}), f32[8,16,128]{2,1,0:T(8,128)S(1)}, u32[]{:S(2)}, u32[]{:S(2)}) async-start(f32[8,16,128]{2,1,0:T(8,128)} %get-tuple-element.8), calls=%async_computation.2 | async-start | bytes 131072 | tf_op jit(solution)/shard_map/all_to_all | solution.py:149
  50.2 13.8 %all-to-all-start.3 = ((bf16[32,16,128]{2,1,0:T(8,128)(2,1)}), bf16[32,16,128]{2,1,0:T(8,128)(2,1)}, u32[]{:S(2)}, u32[]{:S(2)}) async-start(bf16[32,16,128]{2,1,0:T(8,128)(2,1)} %link.1), calls=%async_computation.3 | async-start | bytes 262144 | tf_op jit(solution)/shard_map/all_to_all | solution.py:149
  56.2 7.8 %copy-start = (bf16[128,4096]{1,0:T(8,128)(2,1)S(1)}, bf16[128,4096]{1,0:T(8,128)(2,1)}, u32[]{:S(2)}) copy-start(bf16[128,4096]{1,0:T(8,128)(2,1)} %q_ref.1) | copy-start | bytes 3145732

commit v2 on v1

v2 whole, which is shorter than its diff:
```python
import jax
import jax.numpy as jnp
import ml_dtypes
import numpy as np
from jax import lax
from jax.experimental import pallas as pl
from jax.experimental.pallas import tpu as pltpu
from jax.sharding import PartitionSpec as P

F32, BF16 = jnp.float32, jnp.bfloat16
LANES = 128
SUB = 8
WIDE = SUB * LANES
CHUNK = 128
MODES = 16
NODES = 23
SAMPLES = 24
ROWS = SAMPLES + 2 * MODES
GAIN = SAMPLES - 1


def node_tables():
    half = (CHUNK - 1) / 2.0
    nodes = half + half * np.cos((2.0 * np.arange(NODES) + 1.0) * np.pi / (2.0 * NODES))
    at = np.arange(CHUNK, dtype=np.float64)
    basis = np.zeros((SAMPLES, CHUNK))
    for k in range(NODES):
        others = np.delete(nodes, k)
        basis[k] = np.prod((at[:, None] - others) / (nodes[k] - others), axis=1)
    parts, left = [], basis
    for _ in range(3):
        part = left.astype(ml_dtypes.bfloat16)
        parts.append(part)
        left = left - part.astype(np.float64)
    column = np.concatenate([nodes, np.zeros(SAMPLES - NODES)]).astype(np.float32)
    return [float(n) for n in nodes], np.broadcast_to(column[:, None], (SAMPLES, LANES)), np.concatenate(parts)


def one_minus_exp(x):
    series = jnp.ones_like(x)
    for order in range(9, 1, -1):
        series = 1.0 - x * (1.0 / order) * series
    return jnp.where(x < 0.5, x * series, 1.0 - jnp.exp(-x))


def mode_weights(rate, resid):
    return resid * jnp.sqrt(one_minus_exp(2.0 * rate))


def product(k, v):
    return (k.astype(F32) * v.astype(F32)).astype(BF16)


def tree_sum(terms):
    while len(terms) > 1:
        pairs = [terms[i] + terms[i + 1] for i in range(0, len(terms) - 1, 2)]
        terms = pairs + terms[len(terms) - len(terms) % 2 :]
    return terms[0]


def moments_kernel(k_ref, v_ref, basis_ref, rate_ref, resid_ref, gain_ref, out_ref, par):
    @pl.when(pl.program_id(0) == 0)
    def _():
        rate = rate_ref[...]
        par[0:MODES, :] = rate
        par[MODES : 2 * MODES, :] = mode_weights(rate, resid_ref[...])

    sums = jnp.dot(basis_ref[...], product(k_ref[...], v_ref[...]), preferred_element_type=F32)
    sums = sums[0:SAMPLES] + sums[SAMPLES : 2 * SAMPLES] + sums[2 * SAMPLES :]
    spot = lax.broadcasted_iota(jnp.int32, (SAMPLES, LANES), 0) == GAIN
    gain = jnp.broadcast_to(gain_ref[...], (SAMPLES, LANES))
    for g in range(SUB):
        part = jnp.where(spot, gain, sums[:, g * LANES : (g + 1) * LANES])
        out_ref[g] = jnp.concatenate([part, par[...]], axis=0).astype(BF16)


def mix_kernel(k_ref, v_ref, out_ref):
    for g in range(SUB):
        cols = slice(g * LANES, (g + 1) * LANES)
        out_ref[pl.ds(g, CHUNK, stride=SUB), :] = product(k_ref[:, cols], v_ref[:, cols]).astype(F32)


def block_kernel(nodes, got_ref, rate_ref, before_ref, end_ref):
    rate = rate_ref[...]
    decay = jnp.exp(-float(CHUNK) * rate)
    reach = [jnp.exp(-(CHUNK - 1.0 - node) * rate) for node in nodes]
    state = jnp.zeros((MODES, LANES), F32)
    for d in range(before_ref.shape[0]):
        before_ref[d] = state
        sums = got_ref[d].astype(F32)
        end = tree_sum(
            [reach[k] * jnp.broadcast_to(sums[k : k + 1, :], (MODES, LANES)) for k in range(NODES)]
        )
        state = decay * state + end
    for z in range(end_ref.shape[0]):
        end_ref[z] = state


def link_kernel(place_ref, before_ref, blocks_ref, rate_ref, resid_ref, column_ref, out_ref):
    nchunks = before_ref.shape[0]
    place = place_ref[0]
    rate = rate_ref[...]
    span = jnp.exp(-float(CHUNK * nchunks) * rate)
    start = jnp.zeros((MODES, LANES), F32)
    for z in range(blocks_ref.shape[0]):
        start = jnp.where(z < place, span * start + blocks_ref[z], start)
    decay = jnp.exp(-float(CHUNK) * rate)
    lift = mode_weights(rate, resid_ref[...]) * jnp.exp(-rate)
    column = column_ref[...]
    reach = [
        jnp.exp(-column * jnp.broadcast_to(rate[m : m + 1, :], (SAMPLES, LANES))) for m in range(MODES)
    ]
    for d in range(nchunks):
        lifted = lift * (before_ref[d] + start)
        out_ref[d] = tree_sum(
            [reach[m] * jnp.broadcast_to(lifted[m : m + 1, :], (SAMPLES, LANES)) for m in range(MODES)]
        ).astype(BF16)
        start = decay * start


def inner_kernel(x_ref, got_ref, y_ref, rows, wide):
    for g in range(SUB):
        rows[g * ROWS : (g + 1) * ROWS, :] = got_ref[g].astype(F32)

    def row(place):
        return rows[pl.ds(place, SUB, stride=ROWS), :]

    powers = [jnp.exp(-row(SAMPLES + m)) for m in range(MODES)]
    weights = [row(SAMPLES + MODES + m) for m in range(MODES)]
    gain = row(GAIN)

    def token(t, states):
        at = pl.ds(pl.multiple_of(t * SUB, SUB), SUB)
        x = x_ref[at, :]
        states = tuple(powers[m] * states[m] + x for m in range(MODES))
        wide[at, :] = gain * x + tree_sum([weights[m] * states[m] for m in range(MODES)])
        return states

    zero = jnp.zeros((SUB, LANES), F32)
    lax.fori_loop(0, CHUNK, token, (zero,) * MODES, unroll=4)
    for g in range(SUB):
        y_ref[:, g * LANES : (g + 1) * LANES] = wide[pl.ds(g, CHUNK, stride=SUB), :]


def final_kernel(start_ref, basis_ref, y_ref, q_ref, out_ref):
    values = jnp.concatenate([start_ref[g].astype(F32) for g in range(SUB)], axis=1)
    values = jnp.concatenate([values] * 3, axis=0).astype(BF16)
    pre = y_ref[...] + jnp.dot(basis_ref[...], values, preferred_element_type=F32)
    out_ref[...] = (q_ref[...].astype(F32) * pre.astype(BF16).astype(F32)).astype(BF16)


def local(queries, key_proj, value_proj, decay_rate, residue, skip_gain, *, interpret=False):
    tokens, channels = queries.shape
    groups = channels // LANES
    grid = channels // WIDE
    nseq = lax.axis_size("seq")
    nodes, column, basis = node_tables()

    def call(kernel, name, flops, nbytes, **kw):
        return pl.pallas_call(
            kernel,
            name=name,
            cost_estimate=pl.CostEstimate(flops=flops, bytes_accessed=nbytes, transcendentals=0),
            interpret=interpret,
            **kw,
        )

    def exchange(array, axis):
        return lax.all_to_all(array, axis, split_axis=0, concat_axis=0, tiled=True)

    struct = jax.ShapeDtypeStruct
    tight = pltpu.CompilerParams(vmem_limit_bytes=16 * 1024 * 1024)
    cols = pl.BlockSpec((CHUNK, WIDE), lambda i: (0, i))
    rows = pl.BlockSpec((CHUNK * SUB, LANES), lambda i: (i, 0))

    def fixed(*shape):
        return pl.BlockSpec(shape, lambda i: (0,) * len(shape))

    def stack(depth):
        return pl.BlockSpec((SUB, depth, LANES), lambda i: (i, 0, 0))

    sums = call(
        moments_kernel, "moments", 100_000_000, 3_000_000,
        grid=(grid,),
        in_specs=[
            cols, cols, fixed(3 * SAMPLES, CHUNK),
            fixed(MODES, LANES), fixed(MODES, LANES), fixed(1, LANES),
        ],
        out_specs=stack(ROWS),
        out_shape=struct((groups, ROWS, LANES), BF16),
        scratch_shapes=[pltpu.VMEM((2 * MODES, LANES), F32)],
    )(key_proj, value_proj, jnp.asarray(basis), decay_rate, residue, skip_gain[None, :])
    got = exchange(sums, "ctx")

    mixed = call(
        mix_kernel, "mix", 2_000_000_000, 4_000_000,
        grid=(grid,), in_specs=[cols, cols], out_specs=rows,
        out_shape=struct((grid * CHUNK * SUB, LANES), F32),
        compiler_params=tight,
    )(key_proj, value_proj)

    before, end_state = call(
        lambda *refs: block_kernel(nodes, *refs), "block", 300_000, 500_000,
        grid=(1,),
        in_specs=[fixed(groups, SAMPLES, LANES), fixed(MODES, LANES)],
        out_specs=[fixed(groups, MODES, LANES), fixed(nseq, MODES, LANES)],
        out_shape=[struct((groups, MODES, LANES), F32), struct((nseq, MODES, LANES), F32)],
        compiler_params=tight,
    )(got, decay_rate)
    blocks = exchange(end_state, "seq")

    inner = call(
        inner_kernel, "inner", 2_000_000_000, 5_000_000,
        grid=(grid,), in_specs=[rows, stack(ROWS)], out_specs=cols,
        out_shape=struct((tokens, channels), F32),
        scratch_shapes=[pltpu.VMEM((SUB * ROWS, LANES), F32), pltpu.VMEM((CHUNK * SUB, LANES), F32)],
        compiler_params=tight,
    )(mixed, got)

    starts = call(
        link_kernel, "link", 300_000, 500_000,
        in_specs=[pl.BlockSpec(memory_space=pltpu.SMEM)] + [pl.BlockSpec(memory_space=pltpu.VMEM)] * 5,
        out_shape=struct((groups, SAMPLES, LANES), BF16),
        compiler_params=tight,
    )(
        lax.axis_index("seq").astype(jnp.int32)[None],
        before, blocks, decay_rate, residue, jnp.asarray(column),
    )
    starts = exchange(starts, "ctx")

    return call(
        final_kernel, "final", 100_000_000, 5_000_000,
        grid=(grid,),
        in_specs=[stack(SAMPLES), fixed(CHUNK, 3 * SAMPLES), cols, cols],
        out_specs=cols,
        out_shape=struct((tokens, channels), BF16),
        compiler_params=tight,
    )(starts, jnp.asarray(basis.T), inner, queries)


def solution(mesh):
    rows = P(("seq", "ctx"), None)
    return jax.shard_map(
        local,
        mesh=mesh,
        in_specs=(rows, rows, rows, P(None, "ctx"), P(None, "ctx"), P("ctx")),
        out_specs=rows,
        check_vma=False,
    )
```

time: 69.9 us -> 59 us (0.84)
  starting transfers between devices: 22.8 us -> 13.5 us
  blocking collectives: 11.2 us -> 19.4 us
  waiting for transfers between devices: 15.3 us -> 9.17 us
  Pallas kernels: 17.6 us -> 15.1 us
  local copies, waits for them, and re-layouts: 2.46 us -> 1.32 us
    all_to_all x3 -> x2, starting transfers between devices: 22.8 us -> 13.5 us  [exchange(): return lax.all_to_all(array, axis, split_axis=0, concat_axis=0, tiled=True)]
    all_to_all x1, blocking collectives: 11.2 us -> 19.4 us  [exchange(): return lax.all_to_all(array, axis, split_axis=0, concat_axis=0, tiled=True)]
    all_to_all x3 -> x2, waiting for transfers between devices: 15.3 us -> 9.17 us  [exchange(): return lax.all_to_all(array, axis, split_axis=0, concat_axis=0, tiled=True)]
    pallas_call x4 -> x3, Pallas kernels: 10.1 us -> 7.48 us  [the longest x1 4.02 us: local(): call(moments_kernel, 'moments', 100000000, 3000000, grid=(grid,), in_spec...]
    unnamed x8 -> x14, local copies, waits for them, and re-layouts: 2.46 us -> 1.25 us
  transfers between devices with their start and end apart: 3 -> 2, of which waited for: 3 -> 2; matrix products, arithmetic and copies ran while one was open for 0% -> 0% of each run, Pallas kernels for 10% -> 11%
where the time goes in v2:
time: 59 us; the launch traced here: 58.6 us
  blocking collectives  19.4 us (33%)
  Pallas kernels  15.1 us (26%)
  starting transfers between devices  13.5 us (23%)
  waiting for transfers between devices  9.17 us (16%)
  local copies, waits for them, and re-layouts  1.32 us (2%)
    all_to_all x1, blocking collectives, exchange(): return lax.all_to_all(array, axis, split_axis=0, concat_axis=0, tiled=True)  19.4 us
    all_to_all x2, starting transfers between devices, exchange(): return lax.all_to_all(array, axis, split_axis=0, concat_axis=0, tiled=True)  13.5 us
    all_to_all x2, waiting for transfers between devices, exchange(): return lax.all_to_all(array, axis, split_axis=0, concat_axis=0, tiled=True)  9.17 us
    pallas_call x1, Pallas kernels, local(): call(inner_kernel, 'inner', 2000000000, 5000000, grid=(grid,), in_specs=[...  5.68 us
    pallas_call x1, Pallas kernels, local(): call(moments_kernel, 'moments', 100000000, 3000000, grid=(grid,), in_spec...  4.02 us
    pallas_call x1, Pallas kernels, local(): call(final_kernel, 'final', 100000000, 5000000, grid=(grid,), in_specs=[s...  2.28 us
    unnamed x14, local copies, waits for them, and re-layouts  1.25 us
    pallas_call x1, Pallas kernels, local(): call(link_kernel, 'link', 300000, 500000, in_specs=[pl.BlockSpec(memory_s...  1.23 us
  transfers between devices with their start and end apart: 2, of which 2 were waited for; matrix products, arithmetic and copies ran while one was open for 0% of the time, Pallas kernels for 11%

profile of v2, /device:TPU:1, one launch (start us, length us, event | category | flops | bytes accessed | tf_op | source)
XLA Modules:
  0.0 58.6 jit_solution(12568402235010643963)
XLA Ops:
  0.0 0.0 copy-start.6
  0.0 0.0 copy-start.3
  0.0 0.0 copy-start.5
  0.0 0.0 copy-start
  0.0 0.0 copy-start.1
  0.0 4.0 %moments.1 = bf16[32,56,128]{2,1,0:T(8,128)(2,1)} custom-call(bf16[128,4096]{1,0:T(8,128)(2,1)} %k_ref.3, bf16[128,4096]{1,0:T(8,128)(2,1)} %v_ref.3, bf16[72,128]{1,0:T(8,128)(2,1)} %constant.10.clone.basis_ref, f32[16,128]{1,0:T(8,128)} %rate_ref.3, f32[16,128]{1,0:T(8,128)} %resid_ref.3, f32[1,128]{1,0:T(1,128)} %bitcast.2), custom_call_target="tpu_custom_call" | custom-call | flops 100000000 | bytes 3000000 | tf_op jit(solution)/shard_map/moments/pallas_call | solution.py:182
  4.0 19.4 %all_to_all.15.refs_0_.got_ref = bf16[32,56,128]{2,1,0:T(8,128)(2,1)S(1)} all-to-all(bf16[32,56,128]{2,1,0:T(8,128)(2,1)} %moments.1), channel_id=1, replica_groups=mesh['ctx'=32,'seq'=8] {'ctx'}, dimensions={0} | all-to-all | bytes 917504 | tf_op jit(solution)/shard_map/all_to_all | solution.py:169
  23.5 0.0 copy-done.3
  23.5 1.2 %block.1 = (f32[32,16,128]{2,1,0:T(8,128)S(1)}, f32[8,16,128]{2,1,0:T(8,128)}) custom-call(bf16[32,56,128]{2,1,0:T(8,128)(2,1)S(1)} %all_to_all.15.refs_0_.got_ref, f32[16,128]{1,0:T(8,128)S(1)} %copy-done.3), custom_call_target="tpu_custom_call" | custom-call | flops 300000 | bytes 500000 | tf_op jit(solution)/shard_map/block/pallas_call | solution.py:202
  24.7 8.2 %all-to-all-start.1 = ((f32[8,16,128]{2,1,0:T(8,128)}), f32[8,16,128]{2,1,0:T(8,128)S(1)}, u32[]{:S(2)}, u32[]{:S(2)}) async-start(f32[8,16,128]{2,1,0:T(8,128)} %get-tuple-element.8), calls=%async_computation.1 | async-start | bytes 131072 | tf_op jit(solution)/shard_map/all_to_all | solution.py:169
  32.9 7.2 %all-to-all-done.1.blocks_ref = f32[8,16,128]{2,1,0:T(8,128)S(1)} async-done(((f32[8,16,128]{2,1,0:T(8,128)}), f32[8,16,128]{2,1,0:T(8,128)S(1)}, u32[]{:S(2)}, u32[]{:S(2)}) %all-to-all-start.1) | async-done | bytes 65568 | tf_op jit(solution)/shard_map/all_to_all | solution.py:169
  40.1 0.0 copy-done.6
  40.1 0.1 jit_solution_.3.column_ref
  40.2 0.0 copy-done.5
  40.2 1.2 %link.1 = bf16[32,24,128]{2,1,0:T(8,128)(2,1)} custom-call(s32[1]{0:T(128)} %bitcast.place_ref, f32[32,16,128]{2,1,0:T(8,128)S(1)} %get-tuple-element.7.before_ref, f32[8,16,128]{2,1,0:T(8,128)S(1)} %all-to-all-done.1.blocks_ref, f32[16,128]{1,0:T(8,128)S(1)} %copy-done.3, f32[16,128]{1,0:T(8,128)S(1)} %copy-done.5, f32[24,128]{1,0:T(8,128)S(1)} %jit_solution_.3.column_ref), custom_call_target="tpu_custom_call" | custom-call | flops 300000 | bytes 500000 | tf_op jit(solution)/shard_map/link/pallas_call | solution.py:220
  41.4 5.3 %all-to-all-start.2 = ((bf16[32,24,128]{2,1,0:T(8,128)(2,1)}), bf16[32,24,128]{2,1,0:T(8,128)(2,1)S(1)}, u32[]{:S(2)}, u32[]{:S(2)}) async-start(bf16[32,24,128]{2,1,0:T(8,128)(2,1)} %link.1), calls=%async_computation.2 | async-start | bytes 393216 | tf_op jit(solution)/shard_map/all_to_all | solution.py:169
  46.7 0.0 copy-done
  46.7 0.0 copy-done.1
  46.8 0.7 %mix.1.x_ref = f32[4096,128]{1,0:T(8,128)S(1)} custom-call(bf16[128,4096]{1,0:T(8,128)(2,1)S(1)} %copy-done, bf16[128,4096]{1,0:T(8,128)(2,1)S(1)} %copy-done.1), custom_call_target="tpu_custom_call" | custom-call | flops 2000000000 | bytes 4000000 | tf_op jit(solution)/shard_map/mix/pallas_call | solution.py:195
  47.5 0.0 copy-start.4
  47.5 5.7 %inner.1.y_ref = f32[128,4096]{1,0:T(8,128)S(1)} custom-call(f32[4096,128]{1,0:T(8,128)S(1)} %mix.1.x_ref, bf16[32,56,128]{2,1,0:T(8,128)(2,1)S(1)} %all_to_all.15.refs_0_.got_ref), custom_call_target="tpu_custom_call" | custom-call | flops 2000000000 | bytes 5000000 | tf_op jit(solution)/shard_map/inner/pallas_call | solution.py:212
  53.2 1.9 %all-to-all-done.2.start_ref = bf16[32,24,128]{2,1,0:T(8,128)(2,1)S(1)} async-done(((bf16[32,24,128]{2,1,0:T(8,128)(2,1)}), bf16[32,24,128]{2,1,0:T(8,128)(2,1)S(1)}, u32[]{:S(2)}, u32[]{:S(2)}) %all-to-all-start.2) | async-done | bytes 196640 | tf_op jit(solution)/shard_map/all_to_all | solution.py:169
  55.1 0.0 copy-done.4
  55.1 0.0 copy-start.2
  55.1 1.2 %copy-done.2 = bf16[128,4096]{1,0:T(8,128)(2,1)S(1)} copy-done((bf16[128,4096]{1,0:T(8,128)(2,1)S(1)}, bf16[128,4096]{1,0:T(8,128)(2,1)}, u32[]{:S(2)}) %copy-start.2) | copy-done | bytes 1048600
  56.3 2.3 %final.1 = bf16[128,4096]{1,0:T(8,128)(2,1)} custom-call(bf16[32,24,128]{2,1,0:T(8,128)(2,1)S(1)} %all-to-all-done.2.start_ref, bf16[128,72]{1,0:T(8,128)(2,1)S(1)} %copy-done.4, f32[128,4096]{1,0:T(8,128)S(1)} %inner.1.y_ref, bf16[128,4096]{1,0:T(8,128)(2,1)S(1)} %copy-done.2), custom_call_target="tpu_custom_call" | custom-call | flops 100000000 | bytes 5000000 | tf_op jit(solution)/shard_map/final/pallas_call | solution.py:231
Async XLA Ops:
  0.0 40.1 %copy-start.6 = (f32[24]{0:T(128)S(1)}, f32[24]{0:T(128)}, u32[]{:S(2)}) copy-start(f32[24]{0:T(128)} %constant.11.clone) | copy-start | bytes 292
  0.0 23.5 %copy-start.3 = (f32[16,128]{1,0:T(8,128)S(1)}, f32[16,128]{1,0:T(8,128)}, u32[]{:S(2)}) copy-start(f32[16,128]{1,0:T(8,128)} %rate_ref.3) | copy-start | bytes 24580
  0.0 40.2 %copy-start.5 = (f32[16,128]{1,0:T(8,128)S(1)}, f32[16,128]{1,0:T(8,128)}, u32[]{:S(2)}) copy-start(f32[16,128]{1,0:T(8,128)} %resid_ref.3) | copy-start | bytes 24580
  0.0 46.7 %copy-start = (bf16[128,4096]{1,0:T(8,128)(2,1)S(1)}, bf16[128,4096]{1,0:T(8,128)(2,1)}, u32[]{:S(2)}) copy-start(bf16[128,4096]{1,0:T(8,128)(2,1)} %k_ref.3) | copy-start | bytes 3145732
  0.0 46.7 %copy-start.1 = (bf16[128,4096]{1,0:T(8,128)(2,1)S(1)}, bf16[128,4096]{1,0:T(8,128)(2,1)}, u32[]{:S(2)}) copy-start(bf16[128,4096]{1,0:T(8,128)(2,1)} %v_ref.3) | copy-start | bytes 3145732
  24.7 15.4 %all-to-all-start.1 = ((f32[8,16,128]{2,1,0:T(8,128)}), f32[8,16,128]{2,1,0:T(8,128)S(1)}, u32[]{:S(2)}, u32[]{:S(2)}) async-start(f32[8,16,128]{2,1,0:T(8,128)} %get-tuple-element.8), calls=%async_computation.1 | async-start | bytes 131072 | tf_op jit(solution)/shard_map/all_to_all | solution.py:169
  41.4 13.7 %all-to-all-start.2 = ((bf16[32,24,128]{2,1,0:T(8,128)(2,1)}), bf16[32,24,128]{2,1,0:T(8,128)(2,1)S(1)}, u32[]{:S(2)}, u32[]{:S(2)}) async-start(bf16[32,24,128]{2,1,0:T(8,128)(2,1)} %link.1), calls=%async_computation.2 | async-start | bytes 393216 | tf_op jit(solution)/shard_map/all_to_all | solution.py:169
  47.5 7.6 %copy-start.4 = (bf16[128,72]{1,0:T(8,128)(2,1)S(1)}, bf16[128,72]{1,0:T(8,128)(2,1)}, u32[]{:S(2)}) copy-start(bf16[128,72]{1,0:T(8,128)(2,1)} %constant.12.clone.basis_ref) | copy-start | bytes 55300
  55.1 1.2 %copy-start.2 = (bf16[128,4096]{1,0:T(8,128)(2,1)S(1)}, bf16[128,4096]{1,0:T(8,128)(2,1)}, u32[]{:S(2)}) copy-start(bf16[128,4096]{1,0:T(8,128)(2,1)} %q_ref.1) | copy-start | bytes 3145732

commit v3 on v2

--- a/solution.py
+++ b/solution.py
@@ -11,12 +11,15 @@
 LANES = 128
 SUB = 8
 WIDE = SUB * LANES
+MANY = 16
 CHUNK = 128
 MODES = 16
 NODES = 23
 SAMPLES = 24
 ROWS = SAMPLES + 2 * MODES
 GAIN = SAMPLES - 1
+ROOT_CTX, ROOT_SEQ = 21, 4
+BLOCK_FLIP, GROUP_FLIP, HALF_FLIP = ROOT_CTX // SUB, ROOT_CTX % SUB, ROOT_CTX % MANY
 
 
 def node_tables():
@@ -69,9 +72,9 @@
     sums = sums[0:SAMPLES] + sums[SAMPLES : 2 * SAMPLES] + sums[2 * SAMPLES :]
     spot = lax.broadcasted_iota(jnp.int32, (SAMPLES, LANES), 0) == GAIN
     gain = jnp.broadcast_to(gain_ref[...], (SAMPLES, LANES))
-    for g in range(SUB):
+    for g in range(MANY):
         part = jnp.where(spot, gain, sums[:, g * LANES : (g + 1) * LANES])
-        out_ref[g] = jnp.concatenate([part, par[...]], axis=0).astype(BF16)
+        out_ref[g ^ HALF_FLIP] = jnp.concatenate([part, par[...]], axis=0).astype(BF16)
 
 
 def mix_kernel(k_ref, v_ref, out_ref):
@@ -80,14 +83,14 @@
         out_ref[pl.ds(g, CHUNK, stride=SUB), :] = product(k_ref[:, cols], v_ref[:, cols]).astype(F32)
 
 
-def block_kernel(nodes, got_ref, rate_ref, before_ref, end_ref):
+def block_kernel(nodes, got_ref, rate_ref, after_ref, before_ref, end_ref):
     rate = rate_ref[...]
     decay = jnp.exp(-float(CHUNK) * rate)
     reach = [jnp.exp(-(CHUNK - 1.0 - node) * rate) for node in nodes]
     state = jnp.zeros((MODES, LANES), F32)
     for d in range(before_ref.shape[0]):
         before_ref[d] = state
-        sums = got_ref[d].astype(F32)
+        sums = got_ref[d ^ ROOT_CTX].astype(F32)
         end = tree_sum(
             [reach[k] * jnp.broadcast_to(sums[k : k + 1, :], (MODES, LANES)) for k in range(NODES)]
         )
@@ -96,14 +99,14 @@
         end_ref[z] = state
 
 
-def link_kernel(place_ref, before_ref, blocks_ref, rate_ref, resid_ref, column_ref, out_ref):
+def link_kernel(place_ref, before_ref, blocks_ref, rate_ref, resid_ref, column_ref, after_ref, out_ref):
     nchunks = before_ref.shape[0]
     place = place_ref[0]
     rate = rate_ref[...]
     span = jnp.exp(-float(CHUNK * nchunks) * rate)
     start = jnp.zeros((MODES, LANES), F32)
     for z in range(blocks_ref.shape[0]):
-        start = jnp.where(z < place, span * start + blocks_ref[z], start)
+        start = jnp.where(z < place, span * start + blocks_ref[z ^ ROOT_SEQ], start)
     decay = jnp.exp(-float(CHUNK) * rate)
     lift = mode_weights(rate, resid_ref[...]) * jnp.exp(-rate)
     column = column_ref[...]
@@ -112,15 +115,15 @@
     ]
     for d in range(nchunks):
         lifted = lift * (before_ref[d] + start)
-        out_ref[d] = tree_sum(
+        out_ref[d ^ ROOT_CTX] = tree_sum(
             [reach[m] * jnp.broadcast_to(lifted[m : m + 1, :], (SAMPLES, LANES)) for m in range(MODES)]
         ).astype(BF16)
         start = decay * start
 
 
-def inner_kernel(x_ref, got_ref, y_ref, rows, wide):
+def inner_kernel(x_ref, got_ref, after_ref, held_ref, y_ref, rows, wide):
     for g in range(SUB):
-        rows[g * ROWS : (g + 1) * ROWS, :] = got_ref[g].astype(F32)
+        rows[g * ROWS : (g + 1) * ROWS, :] = got_ref[g ^ GROUP_FLIP].astype(F32)
 
     def row(place):
         return rows[pl.ds(place, SUB, stride=ROWS), :]
@@ -143,7 +146,7 @@
 
 
 def final_kernel(start_ref, basis_ref, y_ref, q_ref, out_ref):
-    values = jnp.concatenate([start_ref[g].astype(F32) for g in range(SUB)], axis=1)
+    values = jnp.concatenate([start_ref[g ^ HALF_FLIP].astype(F32) for g in range(MANY)], axis=1)
     values = jnp.concatenate([values] * 3, axis=0).astype(BF16)
     pre = y_ref[...] + jnp.dot(basis_ref[...], values, preferred_element_type=F32)
     out_ref[...] = (q_ref[...].astype(F32) * pre.astype(BF16).astype(F32)).astype(BF16)
@@ -165,77 +168,102 @@
             **kw,
         )
 
-    def exchange(array, axis):
-        return lax.all_to_all(array, axis, split_axis=0, concat_axis=0, tiled=True)
+    def exchange(array, axis, root):
+        order = [i ^ root for i in range(array.shape[0])]
+        return lax.all_to_all(
+            array, axis, split_axis=0, concat_axis=0, tiled=True, axis_index_groups=[order]
+        )
+
+    def in_hbm(array):
+        return pltpu.with_memory_space_constraint(array, pltpu.HBM)
 
     struct = jax.ShapeDtypeStruct
     tight = pltpu.CompilerParams(vmem_limit_bytes=16 * 1024 * 1024)
-    cols = pl.BlockSpec((CHUNK, WIDE), lambda i: (0, i))
-    rows = pl.BlockSpec((CHUNK * SUB, LANES), lambda i: (i, 0))
+    halves = pl.BlockSpec((CHUNK, MANY * LANES), lambda i: (0, i))
+    anywhere = pl.BlockSpec(memory_space=pl.ANY)
 
     def fixed(*shape):
         return pl.BlockSpec(shape, lambda i: (0,) * len(shape))
 
     def stack(depth):
-        return pl.BlockSpec((SUB, depth, LANES), lambda i: (i, 0, 0))
+        return pl.BlockSpec((MANY, depth, LANES), lambda i: (i ^ (ROOT_CTX // MANY), 0, 0))
 
     sums = call(
         moments_kernel, "moments", 100_000_000, 3_000_000,
-        grid=(grid,),
+        grid=(2,),
         in_specs=[
-            cols, cols, fixed(3 * SAMPLES, CHUNK),
+            halves, halves, fixed(3 * SAMPLES, CHUNK),
             fixed(MODES, LANES), fixed(MODES, LANES), fixed(1, LANES),
         ],
         out_specs=stack(ROWS),
         out_shape=struct((groups, ROWS, LANES), BF16),
         scratch_shapes=[pltpu.VMEM((2 * MODES, LANES), F32)],
     )(key_proj, value_proj, jnp.asarray(basis), decay_rate, residue, skip_gain[None, :])
-    got = exchange(sums, "ctx")
+    got = exchange(sums, "ctx", ROOT_CTX)
 
     mixed = call(
         mix_kernel, "mix", 2_000_000_000, 4_000_000,
-        grid=(grid,), in_specs=[cols, cols], out_specs=rows,
+        grid=(grid,),
+        in_specs=[pl.BlockSpec((CHUNK, WIDE), lambda i: (0, i))] * 2,
+        out_specs=pl.BlockSpec((CHUNK * SUB, LANES), lambda i: (i, 0)),
         out_shape=struct((grid * CHUNK * SUB, LANES), F32),
         compiler_params=tight,
-    )(key_proj, value_proj)
+    )(in_hbm(key_proj), in_hbm(value_proj))
 
     before, end_state = call(
         lambda *refs: block_kernel(nodes, *refs), "block", 300_000, 500_000,
         grid=(1,),
-        in_specs=[fixed(groups, SAMPLES, LANES), fixed(MODES, LANES)],
+        in_specs=[fixed(groups, SAMPLES, LANES), fixed(MODES, LANES), anywhere],
         out_specs=[fixed(groups, MODES, LANES), fixed(nseq, MODES, LANES)],
         out_shape=[struct((groups, MODES, LANES), F32), struct((nseq, MODES, LANES), F32)],
         compiler_params=tight,
-    )(got, decay_rate)
-    blocks = exchange(end_state, "seq")
-
-    inner = call(
-        inner_kernel, "inner", 2_000_000_000, 5_000_000,
-        grid=(grid,), in_specs=[rows, stack(ROWS)], out_specs=cols,
-        out_shape=struct((tokens, channels), F32),
-        scratch_shapes=[pltpu.VMEM((SUB * ROWS, LANES), F32), pltpu.VMEM((CHUNK * SUB, LANES), F32)],
-        compiler_params=tight,
-    )(mixed, got)
+    )(got, decay_rate, mixed)
+    blocks = exchange(end_state, "seq", ROOT_SEQ)
+
+    def respond(half, after, held):
+        steps = grid // 2
+
+        def at(i):
+            return i + half * steps
+
+        specs = [
+            pl.BlockSpec((CHUNK * SUB, LANES), lambda i: (at(i), 0)),
+            pl.BlockSpec((SUB, ROWS, LANES), lambda i: (at(i) ^ BLOCK_FLIP, 0, 0)),
+            anywhere,
+            anywhere,
+        ]
+        return call(
+            inner_kernel, "inner", 1_000_000_000, 2_500_000,
+            grid=(steps,), in_specs=specs,
+            out_specs=pl.BlockSpec((CHUNK, WIDE), lambda i: (0, at(i))),
+            out_shape=struct((tokens, channels), F32),
+            scratch_shapes=[pltpu.VMEM((SUB * ROWS, LANES), F32), pltpu.VMEM((CHUNK * SUB, LANES), F32)],
+            input_output_aliases={3: 0} if half else {},
+            compiler_params=tight,
+        )(mixed, got, after, held)
+
+    inner = respond(0, end_state, end_state)
 
     starts = call(
         link_kernel, "link", 300_000, 500_000,
-        in_specs=[pl.BlockSpec(memory_space=pltpu.SMEM)] + [pl.BlockSpec(memory_space=pltpu.VMEM)] * 5,
+        in_specs=[pl.BlockSpec(memory_space=pltpu.SMEM)] + [pl.BlockSpec(memory_space=pltpu.VMEM)] * 5 + [anywhere],
         out_shape=struct((groups, SAMPLES, LANES), BF16),
         compiler_params=tight,
     )(
         lax.axis_index("seq").astype(jnp.int32)[None],
-        before, blocks, decay_rate, residue, jnp.asarray(column),
+        before, blocks, decay_rate, residue, jnp.asarray(column), inner,
     )
-    starts = exchange(starts, "ctx")
+    inner = respond(1, starts, inner)
+    starts = exchange(starts, "ctx", ROOT_CTX)
 
     return call(
         final_kernel, "final", 100_000_000, 5_000_000,
-        grid=(grid,),
-        in_specs=[stack(SAMPLES), fixed(CHUNK, 3 * SAMPLES), cols, cols],
-        out_specs=cols,
+        grid=(2,),
+        in_specs=[stack(SAMPLES), fixed(CHUNK, 3 * SAMPLES), halves, halves],
+        out_specs=halves,
         out_shape=struct((tokens, channels), BF16),
         compiler_params=tight,
-    )(starts, jnp.asarray(basis.T), inner, queries)
+    )(starts, jnp.asarray(basis.T), inner, in_hbm(queries))
 
 
 def solution(mesh):

time: 59 us -> 51.5 us (0.87)
  blocking collectives: 19.4 us -> 0 us
  starting transfers between devices: 13.5 us -> 28.2 us
  waiting for transfers between devices: 9.17 us -> 3.66 us
  local copies, waits for them, and re-layouts: 1.32 us -> 3.27 us
  Pallas kernels: 15.1 us -> 15.8 us
    all_to_all x1 -> x0, blocking collectives: 19.4 us -> none  [exchange(): return lax.all_to_all(array, axis, split_axis=0, concat_axis=0, tiled=True)]
    all_to_all x2 -> x3, starting transfers between devices: 13.5 us -> 28.2 us  [exchange(): lax.all_to_all(array, axis, split_axis=0, concat_axis=0, tiled=True, axis...]
    all_to_all x2 -> x3, waiting for transfers between devices: 9.17 us -> 3.66 us  [exchange(): lax.all_to_all(array, axis, split_axis=0, concat_axis=0, tiled=True, axis...]
    unnamed x14, local copies, waits for them, and re-layouts: 1.25 us -> 3.2 us
    pallas_call x4 -> x5, Pallas kernels: 12.7 us -> 13.3 us  [the longest x2 5.66 us: respond(): call(inner_kernel, 'inner', 1000000000, 2500000, grid=(steps,), in_specs=...]
  transfers between devices with their start and end apart: 2 -> 3, of which waited for: 2 -> 1; matrix products, arithmetic and copies ran while one was open for 0% -> 0% of each run, Pallas kernels for 11% -> 16%
where the time goes in v3:
time: 51.5 us; the launch traced here: 51 us
  starting transfers between devices  28.2 us (55%)
  Pallas kernels  15.8 us (31%)
  waiting for transfers between devices  3.66 us (7%)
  local copies, waits for them, and re-layouts  3.27 us (6%)
    all_to_all x3, starting transfers between devices, exchange(): lax.all_to_all(array, axis, split_axis=0, concat_axis=0, tiled=True, axis...  28.2 us
    pallas_call x2, Pallas kernels, respond(): call(inner_kernel, 'inner', 1000000000, 2500000, grid=(steps,), in_specs=...  5.66 us
    all_to_all x3, waiting for transfers between devices, exchange(): lax.all_to_all(array, axis, split_axis=0, concat_axis=0, tiled=True, axis...  3.66 us
    unnamed x14, local copies, waits for them, and re-layouts  3.2 us
    pallas_call x1, Pallas kernels, local(): call(moments_kernel, 'moments', 100000000, 3000000, grid=(2,), in_specs=[...  2.57 us
    pallas_call x1, Pallas kernels, local(): call(final_kernel, 'final', 100000000, 5000000, grid=(2,), in_specs=[stac...  2.57 us
    pallas_call x1, Pallas kernels, local(): call(mix_kernel, 'mix', 2000000000, 4000000, grid=(grid,), in_specs=[pl.B...  2.55 us
    pallas_call x1, Pallas kernels, local(): call(link_kernel, 'link', 300000, 500000, in_specs=[pl.BlockSpec(memory_s...  1.24 us
  transfers between devices with their start and end apart: 3, of which 1 were waited for; matrix products, arithmetic and copies ran while one was open for 0% of the time, Pallas kernels for 16%

profile of v3, /device:TPU:1, one launch (start us, length us, event | category | flops | bytes accessed | tf_op | source)
XLA Modules:
  0.0 51.0 jit_solution(9542193180224689811)
XLA Ops:
  0.0 2.6 %moments.1 = bf16[32,56,128]{2,1,0:T(8,128)(2,1)} custom-call(bf16[128,4096]{1,0:T(8,128)(2,1)} %k_ref.3, bf16[128,4096]{1,0:T(8,128)(2,1)} %v_ref.3, bf16[72,128]{1,0:T(8,128)(2,1)} %constant.10.clone.basis_ref, f32[16,128]{1,0:T(8,128)} %rate_ref.3, f32[16,128]{1,0:T(8,128)} %resid_ref.3, f32[1,128]{1,0:T(1,128)} %bitcast.2), custom_call_target="tpu_custom_call" | custom-call | flops 100000000 | bytes 3000000 | tf_op jit(solution)/shard_map/moments/pallas_call | solution.py:191
  2.6 9.9 %all-to-all-start = ((bf16[32,56,128]{2,1,0:T(8,128)(2,1)}), bf16[32,56,128]{2,1,0:T(8,128)(2,1)S(1)}, u32[]{:S(2)}, u32[]{:S(2)}) async-start(bf16[32,56,128]{2,1,0:T(8,128)(2,1)} %moments.1), calls=%async_computation | async-start | bytes 917504 | tf_op jit(solution)/shard_map/all_to_all | solution.py:173
  12.5 0.0 copy-start.3
  12.5 2.5 %mix.1.refs_2_.x_ref = f32[4096,128]{1,0:T(8,128)S(1)} custom-call(bf16[128,4096]{1,0:T(8,128)(2,1)} %k_ref.3, bf16[128,4096]{1,0:T(8,128)(2,1)} %v_ref.3), custom_call_target="tpu_custom_call" | custom-call | flops 2000000000 | bytes 4000000 | tf_op jit(solution)/shard_map/mix/pallas_call | solution.py:204
  15.1 0.0 copy-start
  15.1 3.7 %all-to-all-done.refs_0_.got_ref = bf16[32,56,128]{2,1,0:T(8,128)(2,1)S(1)} async-done(((bf16[32,56,128]{2,1,0:T(8,128)(2,1)}), bf16[32,56,128]{2,1,0:T(8,128)(2,1)S(1)}, u32[]{:S(2)}, u32[]{:S(2)}) %all-to-all-start) | async-done | bytes 458784 | tf_op jit(solution)/shard_map/all_to_all | solution.py:173
  18.8 0.0 copy-done.3
  18.8 1.2 %block.1 = (f32[32,16,128]{2,1,0:T(8,128)S(1)}, f32[8,16,128]{2,1,0:T(8,128)}) custom-call(bf16[32,56,128]{2,1,0:T(8,128)(2,1)S(1)} %all-to-all-done.refs_0_.got_ref, f32[16,128]{1,0:T(8,128)S(1)} %copy-done.3, f32[4096,128]{1,0:T(8,128)S(1)} %mix.1.refs_2_.x_ref), custom_call_target="tpu_custom_call" | custom-call | flops 300000 | bytes 500000 | tf_op jit(solution)/shard_map/block/pallas_call | solution.py:213
  19.9 10.1 %all-to-all-start.1 = ((f32[8,16,128]{2,1,0:T(8,128)}), f32[8,16,128]{2,1,0:T(8,128)S(1)}, u32[]{:S(2)}, u32[]{:S(2)}) async-start(f32[8,16,128]{2,1,0:T(8,128)} %get-tuple-element.8.after_ref.held_ref), calls=%async_computation.1 | async-start | bytes 131072 | tf_op jit(solution)/shard_map/all_to_all | solution.py:173
  30.0 0.0 copy-done
  30.0 0.0 copy-start.1
  30.0 1.6 %copy-done.1 = f32[4096,128]{1,0:T(8,128)S(1)} copy-done((f32[4096,128]{1,0:T(8,128)S(1)}, f32[4096,128]{1,0:T(8,128)}, u32[]{:S(2)}) %copy-start.1) | copy-done | bytes 2097176
  31.6 0.0 copy-start.6
  31.6 0.0 copy-start.5
  31.6 2.8 %inner.2.after_ref.held_ref = f32[128,4096]{1,0:T(8,128)S(1)} custom-call(f32[4096,128]{1,0:T(8,128)S(1)} %copy-done.1, bf16[32,56,128]{2,1,0:T(8,128)(2,1)S(1)} %all-to-all-done.refs_0_.got_ref, f32[8,16,128]{2,1,0:T(8,128)} %get-tuple-element.8.after_ref.held_ref, f32[8,16,128]{2,1,0:T(8,128)} %get-tuple-element.8.after_ref.held_ref), custom_call_target="tpu_custom_call" | custom-call | flops 1000000000 | bytes 2500000 | tf_op jit(solution)/shard_map/inner/pallas_call | solution.py:235
  34.5 0.0 all-to-all-done.1.blocks_ref
  34.5 0.0 copy-done.6
  34.5 0.1 jit_solution_.3.column_ref
  34.6 0.0 copy-done.5
  34.6 1.2 %link.1.after_ref = bf16[32,24,128]{2,1,0:T(8,128)(2,1)} custom-call(s32[1]{0:T(128)} %bitcast.place_ref, f32[32,16,128]{2,1,0:T(8,128)S(1)} %get-tuple-element.7.before_ref, f32[8,16,128]{2,1,0:T(8,128)S(1)} %all-to-all-done.1.blocks_ref, f32[16,128]{1,0:T(8,128)S(1)} %copy-done.3, f32[16,128]{1,0:T(8,128)S(1)} %copy-done.5, ...), custom_call_target="tpu_custom_call" | custom-call | flops 300000 | bytes 500000 | tf_op jit(solution)/shard_map/link/pallas_call | solution.py:247
  35.8 8.2 %all-to-all-start.2 = ((bf16[32,24,128]{2,1,0:T(8,128)(2,1)}), bf16[32,24,128]{2,1,0:T(8,128)(2,1)S(1)}, u32[]{:S(2)}, u32[]{:S(2)}) async-start(bf16[32,24,128]{2,1,0:T(8,128)(2,1)} %link.1.after_ref), calls=%async_computation.2 | async-start | bytes 393216 | tf_op jit(solution)/shard_map/all_to_all | solution.py:173
  44.0 0.0 copy-start.2
  44.0 1.6 %copy-done.2 = f32[4096,128]{1,0:T(8,128)S(1)} copy-done((f32[4096,128]{1,0:T(8,128)S(1)}, f32[4096,128]{1,0:T(8,128)}, u32[]{:S(2)}) %copy-start.2) | copy-done | bytes 2097176
  45.6 0.0 copy-start.4
  45.6 2.8 %inner.3.y_ref = f32[128,4096]{1,0:T(8,128)S(1)} custom-call(f32[4096,128]{1,0:T(8,128)S(1)} %copy-done.2, bf16[32,56,128]{2,1,0:T(8,128)(2,1)S(1)} %all-to-all-done.refs_0_.got_ref, bf16[32,24,128]{2,1,0:T(8,128)(2,1)} %link.1.after_ref, f32[128,4096]{1,0:T(8,128)S(1)} %inner.2.after_ref.held_ref), custom_call_target="tpu_custom_call", output_to_operand_aliasing={{}: (3, {})} | custom-call | flops 1000000000 | bytes 2500000 | tf_op jit(solution)/shard_map/inner/pallas_call | solution.py:235
  48.4 0.0 all-to-all-done.2.start_ref
  48.4 0.0 copy-done.4
  48.4 2.6 %final.1 = bf16[128,4096]{1,0:T(8,128)(2,1)} custom-call(bf16[32,24,128]{2,1,0:T(8,128)(2,1)S(1)} %all-to-all-done.2.start_ref, bf16[128,72]{1,0:T(8,128)(2,1)S(1)} %copy-done.4, f32[128,4096]{1,0:T(8,128)S(1)} %inner.3.y_ref, bf16[128,4096]{1,0:T(8,128)(2,1)} %q_ref.1), custom_call_target="tpu_custom_call" | custom-call | flops 100000000 | bytes 5000000 | tf_op jit(solution)/shard_map/final/pallas_call | solution.py:259
Async XLA Ops:
  2.6 16.2 %all-to-all-start = ((bf16[32,56,128]{2,1,0:T(8,128)(2,1)}), bf16[32,56,128]{2,1,0:T(8,128)(2,1)S(1)}, u32[]{:S(2)}, u32[]{:S(2)}) async-start(bf16[32,56,128]{2,1,0:T(8,128)(2,1)} %moments.1), calls=%async_computation | async-start | bytes 917504 | tf_op jit(solution)/shard_map/all_to_all | solution.py:173
  12.5 6.2 %copy-start.3 = (f32[16,128]{1,0:T(8,128)S(1)}, f32[16,128]{1,0:T(8,128)}, u32[]{:S(2)}) copy-start(f32[16,128]{1,0:T(8,128)} %rate_ref.3) | copy-start | bytes 24580
  15.1 15.0 %copy-start = (f32[4096,128]{1,0:T(8,128)}, f32[4096,128]{1,0:T(8,128)S(1)}, u32[]{:S(2)}) copy-start(f32[4096,128]{1,0:T(8,128)S(1)} %mix.1.refs_2_.x_ref) | copy-start | bytes 6291460
  19.9 14.5 %all-to-all-start.1 = ((f32[8,16,128]{2,1,0:T(8,128)}), f32[8,16,128]{2,1,0:T(8,128)S(1)}, u32[]{:S(2)}, u32[]{:S(2)}) async-start(f32[8,16,128]{2,1,0:T(8,128)} %get-tuple-element.8.after_ref.held_ref), calls=%async_computation.1 | async-start | bytes 131072 | tf_op jit(solution)/shard_map/all_to_all | solution.py:173
  30.0 1.6 %copy-start.1 = (f32[4096,128]{1,0:T(8,128)S(1)}, f32[4096,128]{1,0:T(8,128)}, u32[]{:S(2)}) copy-start(f32[4096,128]{1,0:T(8,128)} %copy-done) | copy-start | bytes 6291460
  31.6 2.9 %copy-start.6 = (f32[24]{0:T(128)S(1)}, f32[24]{0:T(128)}, u32[]{:S(2)}) copy-start(f32[24]{0:T(128)} %constant.11.clone) | copy-start | bytes 292
  31.6 2.9 %copy-start.5 = (f32[16,128]{1,0:T(8,128)S(1)}, f32[16,128]{1,0:T(8,128)}, u32[]{:S(2)}) copy-start(f32[16,128]{1,0:T(8,128)} %resid_ref.3) | copy-start | bytes 24580
  35.8 12.6 %all-to-all-start.2 = ((bf16[32,24,128]{2,1,0:T(8,128)(2,1)}), bf16[32,24,128]{2,1,0:T(8,128)(2,1)S(1)}, u32[]{:S(2)}, u32[]{:S(2)}) async-start(bf16[32,24,128]{2,1,0:T(8,128)(2,1)} %link.1.after_ref), calls=%async_computation.2 | async-start | bytes 393216 | tf_op jit(solution)/shard_map/all_to_all | solution.py:173
  44.0 1.6 %copy-start.2 = (f32[4096,128]{1,0:T(8,128)S(1)}, f32[4096,128]{1,0:T(8,128)}, u32[]{:S(2)}) copy-start(f32[4096,128]{1,0:T(8,128)} %copy-done) | copy-start | bytes 6291460
  45.6 2.9 %copy-start.4 = (bf16[128,72]{1,0:T(8,128)(2,1)S(1)}, bf16[128,72]{1,0:T(8,128)(2,1)}, u32[]{:S(2)}) copy-start(bf16[128,72]{1,0:T(8,128)(2,1)} %constant.12.clone.basis_ref) | copy-start | bytes 55300

commit v4 on v3

--- a/solution.py
+++ b/solution.py
@@ -35,8 +35,7 @@
         part = left.astype(ml_dtypes.bfloat16)
         parts.append(part)
         left = left - part.astype(np.float64)
-    column = np.concatenate([nodes, np.zeros(SAMPLES - NODES)]).astype(np.float32)
-    return [float(n) for n in nodes], np.broadcast_to(column[:, None], (SAMPLES, LANES)), np.concatenate(parts)
+    return [float(n) for n in nodes], np.concatenate(parts)
 
 
 def one_minus_exp(x):
@@ -99,7 +98,7 @@
         end_ref[z] = state
 
 
-def link_kernel(place_ref, before_ref, blocks_ref, rate_ref, resid_ref, column_ref, after_ref, out_ref):
+def link_kernel(nodes, place_ref, before_ref, blocks_ref, rate_ref, resid_ref, after_ref, out_ref):
     nchunks = before_ref.shape[0]
     place = place_ref[0]
     rate = rate_ref[...]
@@ -109,7 +108,10 @@
         start = jnp.where(z < place, span * start + blocks_ref[z ^ ROOT_SEQ], start)
     decay = jnp.exp(-float(CHUNK) * rate)
     lift = mode_weights(rate, resid_ref[...]) * jnp.exp(-rate)
-    column = column_ref[...]
+    spot = lax.broadcasted_iota(jnp.int32, (SAMPLES, LANES), 0)
+    column = jnp.zeros((SAMPLES, LANES), F32)
+    for k, node in enumerate(nodes):
+        column = jnp.where(spot == k, node, column)
     reach = [
         jnp.exp(-column * jnp.broadcast_to(rate[m : m + 1, :], (SAMPLES, LANES))) for m in range(MODES)
     ]
@@ -157,7 +159,7 @@
     groups = channels // LANES
     grid = channels // WIDE
     nseq = lax.axis_size("seq")
-    nodes, column, basis = node_tables()
+    nodes, basis = node_tables()
 
     def call(kernel, name, flops, nbytes, **kw):
         return pl.pallas_call(
@@ -206,8 +208,7 @@
         grid=(grid,),
         in_specs=[pl.BlockSpec((CHUNK, WIDE), lambda i: (0, i))] * 2,
         out_specs=pl.BlockSpec((CHUNK * SUB, LANES), lambda i: (i, 0)),
-        out_shape=struct((grid * CHUNK * SUB, LANES), F32),
-        compiler_params=tight,
+        out_shape=pltpu.HBM((grid * CHUNK * SUB, LANES), F32),
     )(in_hbm(key_proj), in_hbm(value_proj))
 
     before, end_state = call(
@@ -217,7 +218,7 @@
         out_specs=[fixed(groups, MODES, LANES), fixed(nseq, MODES, LANES)],
         out_shape=[struct((groups, MODES, LANES), F32), struct((nseq, MODES, LANES), F32)],
         compiler_params=tight,
-    )(got, decay_rate, mixed)
+    )(got, decay_rate, in_hbm(mixed))
     blocks = exchange(end_state, "seq", ROOT_SEQ)
 
     def respond(half, after, held):
@@ -240,18 +241,18 @@
             scratch_shapes=[pltpu.VMEM((SUB * ROWS, LANES), F32), pltpu.VMEM((CHUNK * SUB, LANES), F32)],
             input_output_aliases={3: 0} if half else {},
             compiler_params=tight,
-        )(mixed, got, after, held)
+        )(in_hbm(mixed), got, after, held)
 
     inner = respond(0, end_state, end_state)
 
     starts = call(
-        link_kernel, "link", 300_000, 500_000,
-        in_specs=[pl.BlockSpec(memory_space=pltpu.SMEM)] + [pl.BlockSpec(memory_space=pltpu.VMEM)] * 5 + [anywhere],
+        lambda *refs: link_kernel(nodes, *refs), "link", 300_000, 500_000,
+        in_specs=[pl.BlockSpec(memory_space=pltpu.SMEM)] + [pl.BlockSpec(memory_space=pltpu.VMEM)] * 4 + [anywhere],
         out_shape=struct((groups, SAMPLES, LANES), BF16),
         compiler_params=tight,
     )(
         lax.axis_index("seq").astype(jnp.int32)[None],
-        before, blocks, decay_rate, residue, jnp.asarray(column), inner,
+        before, blocks, decay_rate, residue, inner,
     )
     inner = respond(1, starts, inner)
     starts = exchange(starts, "ctx", ROOT_CTX)

time: 51.5 us -> 50.4 us (0.979)
  Pallas kernels: 15.8 us -> 19.3 us
  local copies, waits for them, and re-layouts: 3.27 us -> 0.02 us
  waiting for transfers between devices: 3.66 us -> 2.27 us
    unnamed x14 -> x6, local copies, waits for them, and re-layouts: 3.2 us -> 0.02 us
    pallas_call x2, Pallas kernels: 5.66 us -> 7.79 us  [respond(): call(inner_kernel, 'inner', 1000000000, 2500000, grid=(steps,), in_specs=...]
    pallas_call x1, Pallas kernels: 2.55 us -> 3.96 us  [local(): call(mix_kernel, 'mix', 2000000000, 4000000, grid=(grid,), in_specs=[pl.B...]
    all_to_all x3, waiting for transfers between devices: 3.66 us -> 2.27 us  [exchange(): lax.all_to_all(array, axis, split_axis=0, concat_axis=0, tiled=True, axis...]
  transfers between devices with their start and end apart: 3 -> 3, of which waited for: 1 -> 1; matrix products, arithmetic and copies ran while one was open for 0% -> 0% of each run, Pallas kernels for 16% -> 24%
where the time goes in v4:
time: 50.4 us; the launch traced here: 49.9 us
  starting transfers between devices  28.2 us (56%)
  Pallas kernels  19.3 us (38%)
  waiting for transfers between devices  2.27 us (5%)
    all_to_all x3, starting transfers between devices, exchange(): lax.all_to_all(array, axis, split_axis=0, concat_axis=0, tiled=True, axis...  28.2 us
    pallas_call x2, Pallas kernels, respond(): call(inner_kernel, 'inner', 1000000000, 2500000, grid=(steps,), in_specs=...  7.79 us
    pallas_call x1, Pallas kernels, local(): call(mix_kernel, 'mix', 2000000000, 4000000, grid=(grid,), in_specs=[pl.B...  3.96 us
    pallas_call x1, Pallas kernels, local(): call(moments_kernel, 'moments', 100000000, 3000000, grid=(2,), in_specs=[...  2.57 us
    pallas_call x1, Pallas kernels, local(): call(final_kernel, 'final', 100000000, 5000000, grid=(2,), in_specs=[stac...  2.57 us
    all_to_all x3, waiting for transfers between devices, exchange(): lax.all_to_all(array, axis, split_axis=0, concat_axis=0, tiled=True, axis...  2.27 us
    pallas_call x1, Pallas kernels, local(): call(lambda *refs: link_kernel(nodes, *refs), 'link', 300000, 500000, in_...  1.25 us
    pallas_call x1, Pallas kernels, local(): call(lambda *refs: block_kernel(nodes, *refs), 'block', 300000, 500000, g...  1.18 us
  transfers between devices with their start and end apart: 3, of which 1 were waited for; matrix products, arithmetic and copies ran while one was open for 0% of the time, Pallas kernels for 24%

profile of v4, /device:TPU:1, one launch (start us, length us, event | category | flops | bytes accessed | tf_op | source)
XLA Modules:
  0.0 49.9 jit_solution(6464853698785904054)
XLA Ops:
  0.0 2.6 %moments.1 = bf16[32,56,128]{2,1,0:T(8,128)(2,1)} custom-call(bf16[128,4096]{1,0:T(8,128)(2,1)} %k_ref.3, bf16[128,4096]{1,0:T(8,128)(2,1)} %v_ref.3, bf16[72,128]{1,0:T(8,128)(2,1)} %constant.8.clone.basis_ref, f32[16,128]{1,0:T(8,128)} %refs_3_.1, f32[16,128]{1,0:T(8,128)} %refs_4_.1, f32[1,128]{1,0:T(1,128)} %bitcast.2), custom_call_target="tpu_custom_call" | custom-call | flops 100000000 | bytes 3000000 | tf_op jit(solution)/shard_map/moments/pallas_call | solution.py:193
  2.6 9.9 %all-to-all-start = ((bf16[32,56,128]{2,1,0:T(8,128)(2,1)}), bf16[32,56,128]{2,1,0:T(8,128)(2,1)S(1)}, u32[]{:S(2)}, u32[]{:S(2)}) async-start(bf16[32,56,128]{2,1,0:T(8,128)(2,1)} %moments.1), calls=%async_computation | async-start | bytes 917504 | tf_op jit(solution)/shard_map/all_to_all | solution.py:175
  12.5 0.0 copy-start
  12.5 4.0 %mix.1.refs_2_.x_ref = f32[4096,128]{1,0:T(8,128)} custom-call(bf16[128,4096]{1,0:T(8,128)(2,1)} %k_ref.3, bf16[128,4096]{1,0:T(8,128)(2,1)} %v_ref.3), custom_call_target="tpu_custom_call" | custom-call | flops 2000000000 | bytes 4000000 | tf_op jit(solution)/shard_map/mix/pallas_call | solution.py:206
  16.5 2.3 %all-to-all-done.refs_0_.got_ref = bf16[32,56,128]{2,1,0:T(8,128)(2,1)S(1)} async-done(((bf16[32,56,128]{2,1,0:T(8,128)(2,1)}), bf16[32,56,128]{2,1,0:T(8,128)(2,1)S(1)}, u32[]{:S(2)}, u32[]{:S(2)}) %all-to-all-start) | async-done | bytes 458784 | tf_op jit(solution)/shard_map/all_to_all | solution.py:175
  18.8 0.0 copy-done
  18.8 1.2 %block.1 = (f32[32,16,128]{2,1,0:T(8,128)S(1)}, f32[8,16,128]{2,1,0:T(8,128)}) custom-call(bf16[32,56,128]{2,1,0:T(8,128)(2,1)S(1)} %all-to-all-done.refs_0_.got_ref, f32[16,128]{1,0:T(8,128)S(1)} %copy-done, f32[4096,128]{1,0:T(8,128)} %mix.1.refs_2_.x_ref), custom_call_target="tpu_custom_call" | custom-call | flops 300000 | bytes 500000 | tf_op jit(solution)/shard_map/block/pallas_call | solution.py:214
  19.9 10.1 %all-to-all-start.1 = ((f32[8,16,128]{2,1,0:T(8,128)}), f32[8,16,128]{2,1,0:T(8,128)S(1)}, u32[]{:S(2)}, u32[]{:S(2)}) async-start(f32[8,16,128]{2,1,0:T(8,128)} %get-tuple-element.8.after_ref.held_ref), calls=%async_computation.1 | async-start | bytes 131072 | tf_op jit(solution)/shard_map/all_to_all | solution.py:175
  30.0 0.0 copy-start.2
  30.0 3.9 %inner.2.refs_5_.held_ref = f32[128,4096]{1,0:T(8,128)S(1)} custom-call(f32[4096,128]{1,0:T(8,128)} %mix.1.refs_2_.x_ref, bf16[32,56,128]{2,1,0:T(8,128)(2,1)S(1)} %all-to-all-done.refs_0_.got_ref, f32[8,16,128]{2,1,0:T(8,128)} %get-tuple-element.8.after_ref.held_ref, f32[8,16,128]{2,1,0:T(8,128)} %get-tuple-element.8.after_ref.held_ref), custom_call_target="tpu_custom_call" | custom-call | flops 1000000000 | bytes 2500000 | tf_op jit(solution)/shard_map/inner/pallas_call | solution.py:236
  33.9 0.0 all-to-all-done.1.refs_2_
  33.9 0.0 copy-done.2
  34.0 1.3 %link.1.after_ref = bf16[32,24,128]{2,1,0:T(8,128)(2,1)} custom-call(s32[1]{0:T(128)} %bitcast.refs_0_, f32[32,16,128]{2,1,0:T(8,128)S(1)} %get-tuple-element.7.refs_1_, f32[8,16,128]{2,1,0:T(8,128)S(1)} %all-to-all-done.1.refs_2_, f32[16,128]{1,0:T(8,128)S(1)} %copy-done, f32[16,128]{1,0:T(8,128)S(1)} %copy-done.2, f32[128,4096]{1,0:T(8,128)S(1)} %inner.2.refs_5_.held_ref), custom_call_target="tpu_custom_call" | custom-call | flops 300000 | bytes 500000 | tf_op jit(solution)/shard_map/link/pallas_call | solution.py:248
  35.2 8.2 %all-to-all-start.2 = ((bf16[32,24,128]{2,1,0:T(8,128)(2,1)}), bf16[32,24,128]{2,1,0:T(8,128)(2,1)S(1)}, u32[]{:S(2)}, u32[]{:S(2)}) async-start(bf16[32,24,128]{2,1,0:T(8,128)(2,1)} %link.1.after_ref), calls=%async_computation.2 | async-start | bytes 393216 | tf_op jit(solution)/shard_map/all_to_all | solution.py:175
  43.4 0.0 copy-start.1
  43.4 3.9 %inner.3.y_ref = f32[128,4096]{1,0:T(8,128)S(1)} custom-call(f32[4096,128]{1,0:T(8,128)} %mix.1.refs_2_.x_ref, bf16[32,56,128]{2,1,0:T(8,128)(2,1)S(1)} %all-to-all-done.refs_0_.got_ref, bf16[32,24,128]{2,1,0:T(8,128)(2,1)} %link.1.after_ref, f32[128,4096]{1,0:T(8,128)S(1)} %inner.2.refs_5_.held_ref), custom_call_target="tpu_custom_call", output_to_operand_aliasing={{}: (3, {})} | custom-call | flops 1000000000 | bytes 2500000 | tf_op jit(solution)/shard_map/inner/pallas_call | solution.py:236
  47.3 0.0 all-to-all-done.2.start_ref
  47.3 0.0 copy-done.1
  47.3 2.6 %final.1 = bf16[128,4096]{1,0:T(8,128)(2,1)} custom-call(bf16[32,24,128]{2,1,0:T(8,128)(2,1)S(1)} %all-to-all-done.2.start_ref, bf16[128,72]{1,0:T(8,128)(2,1)S(1)} %copy-done.1, f32[128,4096]{1,0:T(8,128)S(1)} %inner.3.y_ref, bf16[128,4096]{1,0:T(8,128)(2,1)} %q_ref.1), custom_call_target="tpu_custom_call" | custom-call | flops 100000000 | bytes 5000000 | tf_op jit(solution)/shard_map/final/pallas_call | solution.py:260
Async XLA Ops:
  2.6 16.2 %all-to-all-start = ((bf16[32,56,128]{2,1,0:T(8,128)(2,1)}), bf16[32,56,128]{2,1,0:T(8,128)(2,1)S(1)}, u32[]{:S(2)}, u32[]{:S(2)}) async-start(bf16[32,56,128]{2,1,0:T(8,128)(2,1)} %moments.1), calls=%async_computation | async-start | bytes 917504 | tf_op jit(solution)/shard_map/all_to_all | solution.py:175
  12.5 6.2 %copy-start = (f32[16,128]{1,0:T(8,128)S(1)}, f32[16,128]{1,0:T(8,128)}, u32[]{:S(2)}) copy-start(f32[16,128]{1,0:T(8,128)} %refs_3_.1) | copy-start | bytes 24580
  19.9 14.0 %all-to-all-start.1 = ((f32[8,16,128]{2,1,0:T(8,128)}), f32[8,16,128]{2,1,0:T(8,128)S(1)}, u32[]{:S(2)}, u32[]{:S(2)}) async-start(f32[8,16,128]{2,1,0:T(8,128)} %get-tuple-element.8.after_ref.held_ref), calls=%async_computation.1 | async-start | bytes 131072 | tf_op jit(solution)/shard_map/all_to_all | solution.py:175
  30.0 3.9 %copy-start.2 = (f32[16,128]{1,0:T(8,128)S(1)}, f32[16,128]{1,0:T(8,128)}, u32[]{:S(2)}) copy-start(f32[16,128]{1,0:T(8,128)} %refs_4_.1) | copy-start | bytes 24580
  35.2 12.1 %all-to-all-start.2 = ((bf16[32,24,128]{2,1,0:T(8,128)(2,1)}), bf16[32,24,128]{2,1,0:T(8,128)(2,1)S(1)}, u32[]{:S(2)}, u32[]{:S(2)}) async-start(bf16[32,24,128]{2,1,0:T(8,128)(2,1)} %link.1.after_ref), calls=%async_computation.2 | async-start | bytes 393216 | tf_op jit(solution)/shard_map/all_to_all | solution.py:175
  43.4 3.9 %copy-start.1 = (bf16[128,72]{1,0:T(8,128)(2,1)S(1)}, bf16[128,72]{1,0:T(8,128)(2,1)}, u32[]{:S(2)}) copy-start(bf16[128,72]{1,0:T(8,128)(2,1)} %constant.9.clone.basis_ref) | copy-start | bytes 55300

commit v5 on v4

--- a/solution.py
+++ b/solution.py
@@ -76,13 +76,14 @@
         out_ref[g ^ HALF_FLIP] = jnp.concatenate([part, par[...]], axis=0).astype(BF16)
 
 
-def mix_kernel(k_ref, v_ref, out_ref):
+def mix_kernel(k_ref, v_ref, out_ref, wide):
     for g in range(SUB):
         cols = slice(g * LANES, (g + 1) * LANES)
-        out_ref[pl.ds(g, CHUNK, stride=SUB), :] = product(k_ref[:, cols], v_ref[:, cols]).astype(F32)
-
-
-def block_kernel(nodes, got_ref, rate_ref, after_ref, before_ref, end_ref):
+        wide[pl.ds(g, CHUNK, stride=SUB), :] = product(k_ref[:, cols], v_ref[:, cols]).astype(F32)
+    out_ref[...] = wide[...].astype(BF16)
+
+
+def block_kernel(nodes, got_ref, rate_ref, after_ref, also_ref, before_ref, end_ref):
     rate = rate_ref[...]
     decay = jnp.exp(-float(CHUNK) * rate)
     reach = [jnp.exp(-(CHUNK - 1.0 - node) * rate) for node in nodes]
@@ -123,7 +124,7 @@
         start = decay * start
 
 
-def inner_kernel(x_ref, got_ref, after_ref, held_ref, y_ref, rows, wide):
+def inner_kernel(x_ref, got_ref, after_ref, y_ref, rows, wide):
     for g in range(SUB):
         rows[g * ROWS : (g + 1) * ROWS, :] = got_ref[g ^ GROUP_FLIP].astype(F32)
 
@@ -134,24 +135,32 @@
     weights = [row(SAMPLES + MODES + m) for m in range(MODES)]
     gain = row(GAIN)
 
-    def token(t, states):
-        at = pl.ds(pl.multiple_of(t * SUB, SUB), SUB)
-        x = x_ref[at, :]
-        states = tuple(powers[m] * states[m] + x for m in range(MODES))
-        wide[at, :] = gain * x + tree_sum([weights[m] * states[m] for m in range(MODES)])
+    def tokens(t, states):
+        at = pl.multiple_of(t * 2 * SUB, 2 * SUB)
+        pair = x_ref[pl.ds(at, 2 * SUB), :].astype(F32)
+        outs = []
+        for x in (pair[:SUB], pair[SUB:]):
+            states = tuple(powers[m] * states[m] + x for m in range(MODES))
+            outs.append(gain * x + tree_sum([weights[m] * states[m] for m in range(MODES)]))
+        wide[pl.ds(at, 2 * SUB), :] = jnp.concatenate(outs, axis=0)
         return states
 
     zero = jnp.zeros((SUB, LANES), F32)
-    lax.fori_loop(0, CHUNK, token, (zero,) * MODES, unroll=4)
+    lax.fori_loop(0, CHUNK // 2, tokens, (zero,) * MODES, unroll=4)
     for g in range(SUB):
         y_ref[:, g * LANES : (g + 1) * LANES] = wide[pl.ds(g, CHUNK, stride=SUB), :]
 
 
-def final_kernel(start_ref, basis_ref, y_ref, q_ref, out_ref):
+def final_kernel(start_ref, basis_ref, first_ref, second_ref, q_ref, out_ref):
     values = jnp.concatenate([start_ref[g ^ HALF_FLIP].astype(F32) for g in range(MANY)], axis=1)
     values = jnp.concatenate([values] * 3, axis=0).astype(BF16)
-    pre = y_ref[...] + jnp.dot(basis_ref[...], values, preferred_element_type=F32)
-    out_ref[...] = (q_ref[...].astype(F32) * pre.astype(BF16).astype(F32)).astype(BF16)
+    carried = jnp.dot(basis_ref[...], values, preferred_element_type=F32)
+    for half, own_ref in enumerate((first_ref, second_ref)):
+
+        @pl.when(pl.program_id(0) == half)
+        def _():
+            pre = own_ref[...] + carried
+            out_ref[...] = (q_ref[...].astype(F32) * pre.astype(BF16).astype(F32)).astype(BF16)
 
 
 def local(queries, key_proj, value_proj, decay_rate, residue, skip_gain, *, interpret=False):
@@ -183,6 +192,7 @@
     tight = pltpu.CompilerParams(vmem_limit_bytes=16 * 1024 * 1024)
     halves = pl.BlockSpec((CHUNK, MANY * LANES), lambda i: (0, i))
     anywhere = pl.BlockSpec(memory_space=pl.ANY)
+    whole = pl.BlockSpec(memory_space=pltpu.VMEM)
 
     def fixed(*shape):
         return pl.BlockSpec(shape, lambda i: (0,) * len(shape))
@@ -203,47 +213,46 @@
     )(key_proj, value_proj, jnp.asarray(basis), decay_rate, residue, skip_gain[None, :])
     got = exchange(sums, "ctx", ROOT_CTX)
 
-    mixed = call(
-        mix_kernel, "mix", 2_000_000_000, 4_000_000,
-        grid=(grid,),
-        in_specs=[pl.BlockSpec((CHUNK, WIDE), lambda i: (0, i))] * 2,
-        out_specs=pl.BlockSpec((CHUNK * SUB, LANES), lambda i: (i, 0)),
-        out_shape=pltpu.HBM((grid * CHUNK * SUB, LANES), F32),
-    )(in_hbm(key_proj), in_hbm(value_proj))
+    def mix(half):
+        return call(
+            mix_kernel, "mix", 1_000_000_000, 2_000_000,
+            grid=(grid // 2,),
+            in_specs=[pl.BlockSpec((CHUNK, WIDE), lambda i: (0, i + half * (grid // 2)))] * 2,
+            out_specs=pl.BlockSpec((CHUNK * SUB, LANES), lambda i: (i, 0)),
+            out_shape=struct((grid // 2 * CHUNK * SUB, LANES), BF16),
+            scratch_shapes=[pltpu.VMEM((CHUNK * SUB, LANES), F32)],
+            compiler_params=tight,
+        )(in_hbm(key_proj), in_hbm(value_proj))
+
+    mixed = [mix(0), mix(1)]
 
     before, end_state = call(
         lambda *refs: block_kernel(nodes, *refs), "block", 300_000, 500_000,
         grid=(1,),
-        in_specs=[fixed(groups, SAMPLES, LANES), fixed(MODES, LANES), anywhere],
+        in_specs=[fixed(groups, SAMPLES, LANES), fixed(MODES, LANES), anywhere, anywhere],
         out_specs=[fixed(groups, MODES, LANES), fixed(nseq, MODES, LANES)],
         out_shape=[struct((groups, MODES, LANES), F32), struct((nseq, MODES, LANES), F32)],
         compiler_params=tight,
-    )(got, decay_rate, in_hbm(mixed))
+    )(got, decay_rate, *mixed)
     blocks = exchange(end_state, "seq", ROOT_SEQ)
 
-    def respond(half, after, held):
+    def respond(half, after):
         steps = grid // 2
-
-        def at(i):
-            return i + half * steps
-
-        specs = [
-            pl.BlockSpec((CHUNK * SUB, LANES), lambda i: (at(i), 0)),
-            pl.BlockSpec((SUB, ROWS, LANES), lambda i: (at(i) ^ BLOCK_FLIP, 0, 0)),
-            anywhere,
-            anywhere,
-        ]
         return call(
             inner_kernel, "inner", 1_000_000_000, 2_500_000,
-            grid=(steps,), in_specs=specs,
-            out_specs=pl.BlockSpec((CHUNK, WIDE), lambda i: (0, at(i))),
-            out_shape=struct((tokens, channels), F32),
+            grid=(steps,),
+            in_specs=[
+                pl.BlockSpec((CHUNK * SUB, LANES), lambda i: (i, 0)),
+                pl.BlockSpec((SUB, ROWS, LANES), lambda i: ((i + half * steps) ^ BLOCK_FLIP, 0, 0)),
+                anywhere,
+            ],
+            out_specs=pl.BlockSpec((CHUNK, WIDE), lambda i: (0, i)),
+            out_shape=struct((tokens, channels // 2), F32),
             scratch_shapes=[pltpu.VMEM((SUB * ROWS, LANES), F32), pltpu.VMEM((CHUNK * SUB, LANES), F32)],
-            input_output_aliases={3: 0} if half else {},
             compiler_params=tight,
-        )(in_hbm(mixed), got, after, held)
-
-    inner = respond(0, end_state, end_state)
+        )(mixed[half], got, after)
+
+    first = respond(0, end_state)
 
     starts = call(
         lambda *refs: link_kernel(nodes, *refs), "link", 300_000, 500_000,
@@ -252,19 +261,19 @@
         compiler_params=tight,
     )(
         lax.axis_index("seq").astype(jnp.int32)[None],
-        before, blocks, decay_rate, residue, inner,
+        before, blocks, decay_rate, residue, first,
     )
-    inner = respond(1, starts, inner)
+    second = respond(1, starts)
     starts = exchange(starts, "ctx", ROOT_CTX)
 
     return call(
         final_kernel, "final", 100_000_000, 5_000_000,
         grid=(2,),
-        in_specs=[stack(SAMPLES), fixed(CHUNK, 3 * SAMPLES), halves, halves],
+        in_specs=[stack(SAMPLES), fixed(CHUNK, 3 * SAMPLES), whole, whole, halves],
         out_specs=halves,
         out_shape=struct((tokens, channels), BF16),
         compiler_params=tight,
-    )(starts, jnp.asarray(basis.T), inner, in_hbm(queries))
+    )(starts, jnp.asarray(basis.T), first, second, in_hbm(queries))
 
 
 def solution(mesh):

time: 50.4 us -> 49.4 us (0.980)
  Pallas kernels: 19.3 us -> 16.4 us
  waiting for transfers between devices: 2.27 us -> 3.93 us
    pallas_call x2, Pallas kernels: 7.79 us -> 5.58 us  [respond(): call(inner_kernel, 'inner', 1000000000, 2500000, grid=(steps,), in_specs=...]
    all_to_all x3, waiting for transfers between devices: 2.27 us -> 3.93 us  [exchange(): lax.all_to_all(array, axis, split_axis=0, concat_axis=0, tiled=True, axis...]
    pallas_call x1 -> x2, Pallas kernels: 3.96 us -> 3.03 us  [mix(): call(mix_kernel, 'mix', 1000000000, 2000000, grid=(grid // 2,), in_specs=...]
  transfers between devices with their start and end apart: 3 -> 3, of which waited for: 1 -> 2; matrix products, arithmetic and copies ran while one was open for 0% -> 0% of each run, Pallas kernels for 24% -> 18%
where the time goes in v5:
time: 49.4 us; the launch traced here: 48.9 us
  starting transfers between devices  28.5 us (58%)
  Pallas kernels  16.4 us (33%)
  waiting for transfers between devices  3.93 us (8%)
    all_to_all x3, starting transfers between devices, exchange(): lax.all_to_all(array, axis, split_axis=0, concat_axis=0, tiled=True, axis...  28.5 us
    pallas_call x2, Pallas kernels, respond(): call(inner_kernel, 'inner', 1000000000, 2500000, grid=(steps,), in_specs=...  5.58 us
    all_to_all x3, waiting for transfers between devices, exchange(): lax.all_to_all(array, axis, split_axis=0, concat_axis=0, tiled=True, axis...  3.93 us
    pallas_call x2, Pallas kernels, mix(): call(mix_kernel, 'mix', 1000000000, 2000000, grid=(grid // 2,), in_specs=...  3.03 us
    pallas_call x1, Pallas kernels, local(): call(final_kernel, 'final', 100000000, 5000000, grid=(2,), in_specs=[stac...  2.76 us
    pallas_call x1, Pallas kernels, local(): call(moments_kernel, 'moments', 100000000, 3000000, grid=(2,), in_specs=[...  2.57 us
    pallas_call x1, Pallas kernels, local(): call(lambda *refs: link_kernel(nodes, *refs), 'link', 300000, 500000, in_...  1.24 us
    pallas_call x1, Pallas kernels, local(): call(lambda *refs: block_kernel(nodes, *refs), 'block', 300000, 500000, g...  1.18 us
  transfers between devices with their start and end apart: 3, of which 2 were waited for; matrix products, arithmetic and copies ran while one was open for 0% of the time, Pallas kernels for 18%

profile of v5, /device:TPU:1, one launch (start us, length us, event | category | flops | bytes accessed | tf_op | source)
XLA Modules:
  0.0 48.9 jit_solution(17772035835282251504)
XLA Ops:
  0.0 2.6 %moments.1 = bf16[32,56,128]{2,1,0:T(8,128)(2,1)} custom-call(bf16[128,4096]{1,0:T(8,128)(2,1)} %k_ref.5, bf16[128,4096]{1,0:T(8,128)(2,1)} %v_ref.5, bf16[72,128]{1,0:T(8,128)(2,1)} %constant.8.clone.basis_ref, f32[16,128]{1,0:T(8,128)} %refs_3_.1, f32[16,128]{1,0:T(8,128)} %refs_4_.1, f32[1,128]{1,0:T(1,128)} %bitcast.2), custom_call_target="tpu_custom_call" | custom-call | flops 100000000 | bytes 3000000 | tf_op jit(solution)/shard_map/moments/pallas_call | solution.py:203
  2.6 9.9 %all-to-all-start = ((bf16[32,56,128]{2,1,0:T(8,128)(2,1)}), bf16[32,56,128]{2,1,0:T(8,128)(2,1)S(1)}, u32[]{:S(2)}, u32[]{:S(2)}) async-start(bf16[32,56,128]{2,1,0:T(8,128)(2,1)} %moments.1), calls=%async_computation | async-start | bytes 917504 | tf_op jit(solution)/shard_map/all_to_all | solution.py:184
  12.5 1.5 %mix.2.refs_2_.x_ref = bf16[2048,128]{1,0:T(8,128)(2,1)S(1)} custom-call(bf16[128,4096]{1,0:T(8,128)(2,1)} %k_ref.5, bf16[128,4096]{1,0:T(8,128)(2,1)} %v_ref.5), custom_call_target="tpu_custom_call" | custom-call | flops 1000000000 | bytes 2000000 | tf_op jit(solution)/shard_map/mix/pallas_call | solution.py:217
  14.0 0.0 copy-start
  14.0 1.5 %mix.3.refs_3_.x_ref = bf16[2048,128]{1,0:T(8,128)(2,1)S(1)} custom-call(bf16[128,4096]{1,0:T(8,128)(2,1)} %k_ref.5, bf16[128,4096]{1,0:T(8,128)(2,1)} %v_ref.5), custom_call_target="tpu_custom_call" | custom-call | flops 1000000000 | bytes 2000000 | tf_op jit(solution)/shard_map/mix/pallas_call | solution.py:217
  15.6 3.2 %all-to-all-done.refs_0_.got_ref = bf16[32,56,128]{2,1,0:T(8,128)(2,1)S(1)} async-done(((bf16[32,56,128]{2,1,0:T(8,128)(2,1)}), bf16[32,56,128]{2,1,0:T(8,128)(2,1)S(1)}, u32[]{:S(2)}, u32[]{:S(2)}) %all-to-all-start) | async-done | bytes 458784 | tf_op jit(solution)/shard_map/all_to_all | solution.py:184
  18.8 0.0 copy-done
  18.8 1.2 %block.1 = (f32[32,16,128]{2,1,0:T(8,128)S(1)}, f32[8,16,128]{2,1,0:T(8,128)}) custom-call(bf16[32,56,128]{2,1,0:T(8,128)(2,1)S(1)} %all-to-all-done.refs_0_.got_ref, f32[16,128]{1,0:T(8,128)S(1)} %copy-done, bf16[2048,128]{1,0:T(8,128)(2,1)S(1)} %mix.2.refs_2_.x_ref, bf16[2048,128]{1,0:T(8,128)(2,1)S(1)} %mix.3.refs_3_.x_ref), custom_call_target="tpu_custom_call" | custom-call | flops 300000 | bytes 500000 | tf_op jit(solution)/shard_map/block/pallas_call | solution.py:229
  19.9 10.1 %all-to-all-start.1 = ((f32[8,16,128]{2,1,0:T(8,128)}), f32[8,16,128]{2,1,0:T(8,128)S(1)}, u32[]{:S(2)}, u32[]{:S(2)}) async-start(f32[8,16,128]{2,1,0:T(8,128)} %get-tuple-element.8.after_ref), calls=%async_computation.1 | async-start | bytes 131072 | tf_op jit(solution)/shard_map/all_to_all | solution.py:184
  30.0 0.0 copy-start.2
  30.0 2.8 %inner.2.refs_5_.first_ref = f32[128,2048]{1,0:T(8,128)S(1)} custom-call(bf16[2048,128]{1,0:T(8,128)(2,1)S(1)} %mix.2.refs_2_.x_ref, bf16[32,56,128]{2,1,0:T(8,128)(2,1)S(1)} %all-to-all-done.refs_0_.got_ref, f32[8,16,128]{2,1,0:T(8,128)} %get-tuple-element.8.after_ref), custom_call_target="tpu_custom_call" | custom-call | flops 1000000000 | bytes 2500000 | tf_op jit(solution)/shard_map/inner/pallas_call | solution.py:241
  32.8 0.0 all-to-all-done.1.refs_2_
  32.8 0.0 copy-done.2
  32.8 1.2 %link.1.after_ref = bf16[32,24,128]{2,1,0:T(8,128)(2,1)} custom-call(s32[1]{0:T(128)} %bitcast.refs_0_, f32[32,16,128]{2,1,0:T(8,128)S(1)} %get-tuple-element.7.refs_1_, f32[8,16,128]{2,1,0:T(8,128)S(1)} %all-to-all-done.1.refs_2_, f32[16,128]{1,0:T(8,128)S(1)} %copy-done, f32[16,128]{1,0:T(8,128)S(1)} %copy-done.2, f32[128,2048]{1,0:T(8,128)S(1)} %inner.2.refs_5_.first_ref), custom_call_target="tpu_custom_call" | custom-call | flops 300000 | bytes 500000 | tf_op jit(solution)/shard_map/link/pallas_call | solution.py:257
  34.1 8.5 %all-to-all-start.2 = ((bf16[32,24,128]{2,1,0:T(8,128)(2,1)}), bf16[32,24,128]{2,1,0:T(8,128)(2,1)S(1)}, u32[]{:S(2)}, u32[]{:S(2)}) async-start(bf16[32,24,128]{2,1,0:T(8,128)(2,1)} %link.1.after_ref), calls=%async_computation.2 | async-start | bytes 393216 | tf_op jit(solution)/shard_map/all_to_all | solution.py:184
  42.6 0.0 copy-start.1
  42.6 2.8 %inner.3.second_ref = f32[128,2048]{1,0:T(8,128)S(1)} custom-call(bf16[2048,128]{1,0:T(8,128)(2,1)S(1)} %mix.3.refs_3_.x_ref, bf16[32,56,128]{2,1,0:T(8,128)(2,1)S(1)} %all-to-all-done.refs_0_.got_ref, bf16[32,24,128]{2,1,0:T(8,128)(2,1)} %link.1.after_ref), custom_call_target="tpu_custom_call" | custom-call | flops 1000000000 | bytes 2500000 | tf_op jit(solution)/shard_map/inner/pallas_call | solution.py:241
  45.4 0.8 %all-to-all-done.2.start_ref = bf16[32,24,128]{2,1,0:T(8,128)(2,1)S(1)} async-done(((bf16[32,24,128]{2,1,0:T(8,128)(2,1)}), bf16[32,24,128]{2,1,0:T(8,128)(2,1)S(1)}, u32[]{:S(2)}, u32[]{:S(2)}) %all-to-all-start.2) | async-done | bytes 196640 | tf_op jit(solution)/shard_map/all_to_all | solution.py:184
  46.2 0.0 copy-done.1
  46.2 2.8 %final.1 = bf16[128,4096]{1,0:T(8,128)(2,1)} custom-call(bf16[32,24,128]{2,1,0:T(8,128)(2,1)S(1)} %all-to-all-done.2.start_ref, bf16[128,72]{1,0:T(8,128)(2,1)S(1)} %copy-done.1, f32[128,2048]{1,0:T(8,128)S(1)} %inner.2.refs_5_.first_ref, f32[128,2048]{1,0:T(8,128)S(1)} %inner.3.second_ref, bf16[128,4096]{1,0:T(8,128)(2,1)} %q_ref.1), custom_call_target="tpu_custom_call" | custom-call | flops 100000000 | bytes 5000000 | tf_op jit(solution)/shard_map/final/pallas_call | solution.py:269
Async XLA Ops:
  2.6 16.2 %all-to-all-start = ((bf16[32,56,128]{2,1,0:T(8,128)(2,1)}), bf16[32,56,128]{2,1,0:T(8,128)(2,1)S(1)}, u32[]{:S(2)}, u32[]{:S(2)}) async-start(bf16[32,56,128]{2,1,0:T(8,128)(2,1)} %moments.1), calls=%async_computation | async-start | bytes 917504 | tf_op jit(solution)/shard_map/all_to_all | solution.py:184
  14.0 4.7 %copy-start = (f32[16,128]{1,0:T(8,128)S(1)}, f32[16,128]{1,0:T(8,128)}, u32[]{:S(2)}) copy-start(f32[16,128]{1,0:T(8,128)} %refs_3_.1) | copy-start | bytes 24580
  19.9 12.9 %all-to-all-start.1 = ((f32[8,16,128]{2,1,0:T(8,128)}), f32[8,16,128]{2,1,0:T(8,128)S(1)}, u32[]{:S(2)}, u32[]{:S(2)}) async-start(f32[8,16,128]{2,1,0:T(8,128)} %get-tuple-element.8.after_ref), calls=%async_computation.1 | async-start | bytes 131072 | tf_op jit(solution)/shard_map/all_to_all | solution.py:184
  30.0 2.8 %copy-start.2 = (f32[16,128]{1,0:T(8,128)S(1)}, f32[16,128]{1,0:T(8,128)}, u32[]{:S(2)}) copy-start(f32[16,128]{1,0:T(8,128)} %refs_4_.1) | copy-start | bytes 24580
  34.1 12.1 %all-to-all-start.2 = ((bf16[32,24,128]{2,1,0:T(8,128)(2,1)}), bf16[32,24,128]{2,1,0:T(8,128)(2,1)S(1)}, u32[]{:S(2)}, u32[]{:S(2)}) async-start(bf16[32,24,128]{2,1,0:T(8,128)(2,1)} %link.1.after_ref), calls=%async_computation.2 | async-start | bytes 393216 | tf_op jit(solution)/shard_map/all_to_all | solution.py:184
  42.6 3.6 %copy-start.1 = (bf16[128,72]{1,0:T(8,128)(2,1)S(1)}, bf16[128,72]{1,0:T(8,128)(2,1)}, u32[]{:S(2)}) copy-start(bf16[128,72]{1,0:T(8,128)(2,1)} %constant.9.clone.basis_ref) | copy-start | bytes 55300

commit v6 on v5

--- a/solution.py
+++ b/solution.py
@@ -90,7 +90,7 @@
     state = jnp.zeros((MODES, LANES), F32)
     for d in range(before_ref.shape[0]):
         before_ref[d] = state
-        sums = got_ref[d ^ ROOT_CTX].astype(F32)
+        sums = got_ref[d ^ ROOT_CTX, 0:SAMPLES, :].astype(F32)
         end = tree_sum(
             [reach[k] * jnp.broadcast_to(sums[k : k + 1, :], (MODES, LANES)) for k in range(NODES)]
         )
@@ -229,7 +229,7 @@
     before, end_state = call(
         lambda *refs: block_kernel(nodes, *refs), "block", 300_000, 500_000,
         grid=(1,),
-        in_specs=[fixed(groups, SAMPLES, LANES), fixed(MODES, LANES), anywhere, anywhere],
+        in_specs=[whole, fixed(MODES, LANES), anywhere, anywhere],
         out_specs=[fixed(groups, MODES, LANES), fixed(nseq, MODES, LANES)],
         out_shape=[struct((groups, MODES, LANES), F32), struct((nseq, MODES, LANES), F32)],
         compiler_params=tight,

time: 49.4 us -> 49.4 us (level)
  no operation moved by 1% of the time
where the time goes in v6:
time: 49.4 us; the launch traced here: 49 us
  starting transfers between devices  28.5 us (58%)
  Pallas kernels  16.5 us (33%)
  waiting for transfers between devices  3.93 us (8%)
    all_to_all x3, starting transfers between devices, exchange(): lax.all_to_all(array, axis, split_axis=0, concat_axis=0, tiled=True, axis...  28.5 us
    pallas_call x2, Pallas kernels, respond(): call(inner_kernel, 'inner', 1000000000, 2500000, grid=(steps,), in_specs=...  5.58 us
    all_to_all x3, waiting for transfers between devices, exchange(): lax.all_to_all(array, axis, split_axis=0, concat_axis=0, tiled=True, axis...  3.93 us
    pallas_call x2, Pallas kernels, mix(): call(mix_kernel, 'mix', 1000000000, 2000000, grid=(grid // 2,), in_specs=...  3.03 us
    pallas_call x1, Pallas kernels, local(): call(final_kernel, 'final', 100000000, 5000000, grid=(2,), in_specs=[stac...  2.76 us
    pallas_call x1, Pallas kernels, local(): call(moments_kernel, 'moments', 100000000, 3000000, grid=(2,), in_specs=[...  2.57 us
    pallas_call x1, Pallas kernels, local(): call(lambda *refs: block_kernel(nodes, *refs), 'block', 300000, 500000, g...  1.27 us
    pallas_call x1, Pallas kernels, local(): call(lambda *refs: link_kernel(nodes, *refs), 'link', 300000, 500000, in_...  1.24 us
  transfers between devices with their start and end apart: 3, of which 2 were waited for; matrix products, arithmetic and copies ran while one was open for 0% of the time, Pallas kernels for 18%

profile of v6, /device:TPU:1, one launch (start us, length us, event | category | flops | bytes accessed | tf_op | source)
XLA Modules:
  0.0 49.0 jit_solution(7979549845446782212)
XLA Ops:
  0.0 2.6 %moments.1 = bf16[32,56,128]{2,1,0:T(8,128)(2,1)} custom-call(bf16[128,4096]{1,0:T(8,128)(2,1)} %k_ref.5, bf16[128,4096]{1,0:T(8,128)(2,1)} %v_ref.5, bf16[72,128]{1,0:T(8,128)(2,1)} %constant.8.clone.basis_ref, f32[16,128]{1,0:T(8,128)} %refs_3_.1, f32[16,128]{1,0:T(8,128)} %refs_4_.1, f32[1,128]{1,0:T(1,128)} %bitcast.2), custom_call_target="tpu_custom_call" | custom-call | flops 100000000 | bytes 3000000 | tf_op jit(solution)/shard_map/moments/pallas_call | solution.py:203
  2.6 9.9 %all-to-all-start = ((bf16[32,56,128]{2,1,0:T(8,128)(2,1)}), bf16[32,56,128]{2,1,0:T(8,128)(2,1)S(1)}, u32[]{:S(2)}, u32[]{:S(2)}) async-start(bf16[32,56,128]{2,1,0:T(8,128)(2,1)} %moments.1), calls=%async_computation | async-start | bytes 917504 | tf_op jit(solution)/shard_map/all_to_all | solution.py:184
  12.5 1.5 %mix.2.refs_2_.x_ref = bf16[2048,128]{1,0:T(8,128)(2,1)S(1)} custom-call(bf16[128,4096]{1,0:T(8,128)(2,1)} %k_ref.5, bf16[128,4096]{1,0:T(8,128)(2,1)} %v_ref.5), custom_call_target="tpu_custom_call" | custom-call | flops 1000000000 | bytes 2000000 | tf_op jit(solution)/shard_map/mix/pallas_call | solution.py:217
  14.0 0.0 copy-start
  14.0 1.5 %mix.3.refs_3_.x_ref = bf16[2048,128]{1,0:T(8,128)(2,1)S(1)} custom-call(bf16[128,4096]{1,0:T(8,128)(2,1)} %k_ref.5, bf16[128,4096]{1,0:T(8,128)(2,1)} %v_ref.5), custom_call_target="tpu_custom_call" | custom-call | flops 1000000000 | bytes 2000000 | tf_op jit(solution)/shard_map/mix/pallas_call | solution.py:217
  15.6 3.2 %all-to-all-done.refs_0_.got_ref = bf16[32,56,128]{2,1,0:T(8,128)(2,1)S(1)} async-done(((bf16[32,56,128]{2,1,0:T(8,128)(2,1)}), bf16[32,56,128]{2,1,0:T(8,128)(2,1)S(1)}, u32[]{:S(2)}, u32[]{:S(2)}) %all-to-all-start) | async-done | bytes 458784 | tf_op jit(solution)/shard_map/all_to_all | solution.py:184
  18.8 0.0 copy-done
  18.8 1.3 %block.1 = (f32[32,16,128]{2,1,0:T(8,128)S(1)}, f32[8,16,128]{2,1,0:T(8,128)}) custom-call(bf16[32,56,128]{2,1,0:T(8,128)(2,1)S(1)} %all-to-all-done.refs_0_.got_ref, f32[16,128]{1,0:T(8,128)S(1)} %copy-done, bf16[2048,128]{1,0:T(8,128)(2,1)S(1)} %mix.2.refs_2_.x_ref, bf16[2048,128]{1,0:T(8,128)(2,1)S(1)} %mix.3.refs_3_.x_ref), custom_call_target="tpu_custom_call" | custom-call | flops 300000 | bytes 500000 | tf_op jit(solution)/shard_map/block/pallas_call | solution.py:229
  20.0 10.1 %all-to-all-start.1 = ((f32[8,16,128]{2,1,0:T(8,128)}), f32[8,16,128]{2,1,0:T(8,128)S(1)}, u32[]{:S(2)}, u32[]{:S(2)}) async-start(f32[8,16,128]{2,1,0:T(8,128)} %get-tuple-element.8.after_ref), calls=%async_computation.1 | async-start | bytes 131072 | tf_op jit(solution)/shard_map/all_to_all | solution.py:184
  30.1 0.0 copy-start.2
  30.1 2.8 %inner.2.refs_5_.first_ref = f32[128,2048]{1,0:T(8,128)S(1)} custom-call(bf16[2048,128]{1,0:T(8,128)(2,1)S(1)} %mix.2.refs_2_.x_ref, bf16[32,56,128]{2,1,0:T(8,128)(2,1)S(1)} %all-to-all-done.refs_0_.got_ref, f32[8,16,128]{2,1,0:T(8,128)} %get-tuple-element.8.after_ref), custom_call_target="tpu_custom_call" | custom-call | flops 1000000000 | bytes 2500000 | tf_op jit(solution)/shard_map/inner/pallas_call | solution.py:241
  32.9 0.0 all-to-all-done.1.refs_2_
  32.9 0.0 copy-done.2
  32.9 1.2 %link.1.after_ref = bf16[32,24,128]{2,1,0:T(8,128)(2,1)} custom-call(s32[1]{0:T(128)} %bitcast.refs_0_, f32[32,16,128]{2,1,0:T(8,128)S(1)} %get-tuple-element.7.refs_1_, f32[8,16,128]{2,1,0:T(8,128)S(1)} %all-to-all-done.1.refs_2_, f32[16,128]{1,0:T(8,128)S(1)} %copy-done, f32[16,128]{1,0:T(8,128)S(1)} %copy-done.2, f32[128,2048]{1,0:T(8,128)S(1)} %inner.2.refs_5_.first_ref), custom_call_target="tpu_custom_call" | custom-call | flops 300000 | bytes 500000 | tf_op jit(solution)/shard_map/link/pallas_call | solution.py:257
  34.2 8.5 %all-to-all-start.2 = ((bf16[32,24,128]{2,1,0:T(8,128)(2,1)}), bf16[32,24,128]{2,1,0:T(8,128)(2,1)S(1)}, u32[]{:S(2)}, u32[]{:S(2)}) async-start(bf16[32,24,128]{2,1,0:T(8,128)(2,1)} %link.1.after_ref), calls=%async_computation.2 | async-start | bytes 393216 | tf_op jit(solution)/shard_map/all_to_all | solution.py:184
  42.7 0.0 copy-start.1
  42.7 2.8 %inner.3.second_ref = f32[128,2048]{1,0:T(8,128)S(1)} custom-call(bf16[2048,128]{1,0:T(8,128)(2,1)S(1)} %mix.3.refs_3_.x_ref, bf16[32,56,128]{2,1,0:T(8,128)(2,1)S(1)} %all-to-all-done.refs_0_.got_ref, bf16[32,24,128]{2,1,0:T(8,128)(2,1)} %link.1.after_ref), custom_call_target="tpu_custom_call" | custom-call | flops 1000000000 | bytes 2500000 | tf_op jit(solution)/shard_map/inner/pallas_call | solution.py:241
  45.5 0.8 %all-to-all-done.2.start_ref = bf16[32,24,128]{2,1,0:T(8,128)(2,1)S(1)} async-done(((bf16[32,24,128]{2,1,0:T(8,128)(2,1)}), bf16[32,24,128]{2,1,0:T(8,128)(2,1)S(1)}, u32[]{:S(2)}, u32[]{:S(2)}) %all-to-all-start.2) | async-done | bytes 196640 | tf_op jit(solution)/shard_map/all_to_all | solution.py:184
  46.3 0.0 copy-done.1
  46.3 2.8 %final.1 = bf16[128,4096]{1,0:T(8,128)(2,1)} custom-call(bf16[32,24,128]{2,1,0:T(8,128)(2,1)S(1)} %all-to-all-done.2.start_ref, bf16[128,72]{1,0:T(8,128)(2,1)S(1)} %copy-done.1, f32[128,2048]{1,0:T(8,128)S(1)} %inner.2.refs_5_.first_ref, f32[128,2048]{1,0:T(8,128)S(1)} %inner.3.second_ref, bf16[128,4096]{1,0:T(8,128)(2,1)} %q_ref.1), custom_call_target="tpu_custom_call" | custom-call | flops 100000000 | bytes 5000000 | tf_op jit(solution)/shard_map/final/pallas_call | solution.py:269
Async XLA Ops:
  2.6 16.2 %all-to-all-start = ((bf16[32,56,128]{2,1,0:T(8,128)(2,1)}), bf16[32,56,128]{2,1,0:T(8,128)(2,1)S(1)}, u32[]{:S(2)}, u32[]{:S(2)}) async-start(bf16[32,56,128]{2,1,0:T(8,128)(2,1)} %moments.1), calls=%async_computation | async-start | bytes 917504 | tf_op jit(solution)/shard_map/all_to_all | solution.py:184
  14.0 4.7 %copy-start = (f32[16,128]{1,0:T(8,128)S(1)}, f32[16,128]{1,0:T(8,128)}, u32[]{:S(2)}) copy-start(f32[16,128]{1,0:T(8,128)} %refs_3_.1) | copy-start | bytes 24580
  20.0 12.9 %all-to-all-start.1 = ((f32[8,16,128]{2,1,0:T(8,128)}), f32[8,16,128]{2,1,0:T(8,128)S(1)}, u32[]{:S(2)}, u32[]{:S(2)}) async-start(f32[8,16,128]{2,1,0:T(8,128)} %get-tuple-element.8.after_ref), calls=%async_computation.1 | async-start | bytes 131072 | tf_op jit(solution)/shard_map/all_to_all | solution.py:184
  30.1 2.8 %copy-start.2 = (f32[16,128]{1,0:T(8,128)S(1)}, f32[16,128]{1,0:T(8,128)}, u32[]{:S(2)}) copy-start(f32[16,128]{1,0:T(8,128)} %refs_4_.1) | copy-start | bytes 24580
  34.2 12.1 %all-to-all-start.2 = ((bf16[32,24,128]{2,1,0:T(8,128)(2,1)}), bf16[32,24,128]{2,1,0:T(8,128)(2,1)S(1)}, u32[]{:S(2)}, u32[]{:S(2)}) async-start(bf16[32,24,128]{2,1,0:T(8,128)(2,1)} %link.1.after_ref), calls=%async_computation.2 | async-start | bytes 393216 | tf_op jit(solution)/shard_map/all_to_all | solution.py:184
  42.7 3.6 %copy-start.1 = (bf16[128,72]{1,0:T(8,128)(2,1)S(1)}, bf16[128,72]{1,0:T(8,128)(2,1)}, u32[]{:S(2)}) copy-start(bf16[128,72]{1,0:T(8,128)(2,1)} %constant.9.clone.basis_ref) | copy-start | bytes 55300
